TPU v7x, 32 devices: a whole 2x2x4 slice. The times are simulated.
32 devices in a mesh: experts: 4 (over z), context: 4 (over y, x), dp: 2 (over core).
Axes of the slice: x: 2, y: 2, z: 4, core: 2. Of those that a mesh axis runs over, the one named last changes fastest.
Arguments:
- tokens: bfloat16 [8, 4096, 512], P(('experts', 'dp'), 'context'), may hold values from -6 to 6
- attn_gain: float32 [512], replicated, may hold values from 0.5 to 1.5
- mix_gain: float32 [512], replicated, may hold values from 0.5 to 1.5
- query_key_value_weight: bfloat16 [512, 1536], replicated, may hold values from -0.375 to 0.375
- output_weight: bfloat16 [512, 512], replicated, may hold values from -0.75 to 0.75
- router_weight: bfloat16 [512, 8], replicated, may hold values from -0.1875 to 0.1875
- w_in: bfloat16 [8, 512, 2048], P('experts'), may hold values from -1.5 to 1.5
- w_exp_out: bfloat16 [8, 2048, 512], P('experts'), may hold values from -1 to 1
- out_grad: bfloat16 [8, 4096, 512], P(('experts', 'dp'), 'context'), may hold values from -6 to 6
- group_slot: int32 [8, 4096], P(('experts', 'dp'), 'context'), may hold values from 0 to 1023, as said below
- group_routes: int32 [1024, 4], P(('experts', 'context', 'dp')), may hold values from 0 to 7, all different within a row
- route_order: int32 [1024, 4], P(('experts', 'context', 'dp')), may hold values from 0 to 127, as said below
Outputs:
- layer_out: bfloat16 [8, 4096, 512], P(('experts', 'dp'), 'context')
- token_grad: float32 [8, 4096, 512], P(('experts', 'dp'), 'context')
- attn_gain_grad: float32 [512], replicated
- mix_gain_grad: float32 [512], replicated
- qkv_grad: float32 [512, 1536], replicated
- out_proj_grad: float32 [512, 512], replicated
- route_grad: float32 [512, 8], replicated
- expert_in_grad: float32 [8, 512, 2048], P('experts')
- expert_out_grad: float32 [8, 2048, 512], P('experts')
Inputs may be any that keep to these rules, and one draw needn't show every extreme that they name: `group_slot`: in each run of 1024 positions c * 1024 to c * 1024 + 1023 of a sequence, every slot appears exactly once. `group_routes`: each row names 4 different experts; every expert is named by some row. `route_order`: in each aligned block of 32 rows, all 128 entries differ.
All inputs are finite; a program needn't handle non-finite values.
Results may differ from a plain program's by a relative error of at most 0.028.
Values may be sent and summed in bfloat16 or wider, within the bound.
A program may use at most 256 MiB of HBM per device.

v0:
```python
from functools import partial
import math

import jax
import jax.numpy as jnp
from jax import lax
from jax.sharding import PartitionSpec as P

HEADS = 8


NORM_EPS = 1e-05
MASKED = -1e30


def passed_along(block, axis, distance):
    devices = range(lax.axis_size(axis))
    route = [((i - distance) % len(devices), i) for i in devices]
    return lax.ppermute(block, axis, route)


def smooth_gate(values):
    return jax.nn.gelu(values, approximate=True)


def norm_forward(values, gain):
    inv_rms = lax.rsqrt(jnp.mean(values * values, axis=-1, keepdims=True) + NORM_EPS)
    return (values * inv_rms * gain, inv_rms)


def norm_backward(values, inv_rms, gain, grad_normed):
    normed = values * inv_rms
    scaled_grad = grad_normed * gain
    gain_grad = jnp.sum(grad_normed * normed, axis=0)
    inner_mean = jnp.mean(scaled_grad * normed, axis=-1, keepdims=True)
    return (inv_rms * (scaled_grad - normed * inner_mean), gain_grad)


def place_pairs(route_flat, order_flat, capacity, experts):
    same_expert = route_flat[:, None] == route_flat[None, :]
    earlier = order_flat[None, :] < order_flat[:, None]
    ranks = jnp.sum((same_expert & earlier).astype(jnp.int32), axis=1)
    return jnp.where(ranks < capacity, route_flat * capacity + ranks, experts * capacity)


def split_heads(matrix, head_count):
    return matrix.reshape(matrix.shape[0], head_count, matrix.shape[1] // head_count)


def fold_keys(carried_in, keyval, first_key, queries, first_query, block_keys):
    half_width = keyval.shape[1] // 2
    head_count = queries.shape[1]
    query_rows = queries.shape[0]
    score_scale = queries.shape[2] ** (-0.5)
    query_pos = first_query + jnp.arange(query_rows)
    block_count = jnp.clip(
        (first_query + query_rows + block_keys - 1) // block_keys, 0, keyval.shape[0] // block_keys
    )

    def fold_visit_block(step_index, carried):
        run_peak, run_total, run_accum = carried
        kv_block = lax.dynamic_slice_in_dim(keyval, step_index * block_keys, block_keys, 0)
        key_heads = split_heads(kv_block[:, :half_width], head_count)
        value_heads = split_heads(kv_block[:, half_width:], head_count)
        scores = (
            jnp.einsum("qhd,khd->hqk", queries, key_heads, preferred_element_type=jnp.float32)
            * score_scale
        )
        key_pos = step_index * block_keys + jnp.arange(block_keys)
        allowed = key_pos[None, None, :] <= query_pos[None, :, None]
        scores = jnp.where(allowed, scores, MASKED)
        new_peak = jnp.maximum(run_peak, jnp.max(scores, axis=-1))
        weights = jnp.where(allowed, jnp.exp(scores - new_peak[:, :, None]), 0.0)
        factor = jnp.exp(run_peak - new_peak)
        run_total = run_total * factor + jnp.sum(weights, axis=-1)
        update = jnp.einsum(
            "hqk,khd->qhd",
            weights.astype(jnp.bfloat16),
            value_heads,
            preferred_element_type=jnp.float32,
        )
        run_accum = run_accum * jnp.transpose(factor)[:, :, None] + update
        return (new_peak, run_total, run_accum)

    return lax.fori_loop(0, block_count, fold_visit_block, carried_in)


def back_keys(gathered, queries, grad_heads, delta_rows, log_total, first_query, block_keys):
    half_width = gathered.shape[1] // 2
    head_count = queries.shape[1]
    query_rows = queries.shape[0]
    score_scale = queries.shape[2] ** (-0.5)
    query_pos = first_query + jnp.arange(query_rows)
    block_count = (first_query + query_rows + block_keys - 1) // block_keys

    def back_visit_block(step_index, carried):
        grad_query, grad_keyval = carried
        kv_block = lax.dynamic_slice_in_dim(gathered, step_index * block_keys, block_keys, 0)
        key_heads = split_heads(kv_block[:, :half_width], head_count)
        value_heads = split_heads(kv_block[:, half_width:], head_count)
        scores = (
            jnp.einsum("qhd,khd->hqk", queries, key_heads, preferred_element_type=jnp.float32)
            * score_scale
        )
        key_pos = step_index * block_keys + jnp.arange(block_keys)
        allowed = key_pos[None, None, :] <= query_pos[None, :, None]
        probs_full = jnp.where(allowed, jnp.exp(scores - log_total[:, :, None]), 0.0)
        grad_value = jnp.einsum(
            "hqk,qhd->khd",
            probs_full.astype(jnp.bfloat16),
            grad_heads,
            preferred_element_type=jnp.float32,
        )
        grad_probs = jnp.einsum(
            "qhd,khd->hqk", grad_heads, value_heads, preferred_element_type=jnp.float32
        )
        grad_scores = (probs_full * (grad_probs - delta_rows[:, :, None])).astype(jnp.bfloat16)
        grad_query = (
            grad_query
            + jnp.einsum("hqk,khd->qhd", grad_scores, key_heads, preferred_element_type=jnp.float32)
            * score_scale
        )
        grad_key = (
            jnp.einsum("hqk,qhd->khd", grad_scores, queries, preferred_element_type=jnp.float32)
            * score_scale
        )
        merged = jnp.concatenate(
            [grad_key.reshape(block_keys, half_width), grad_value.reshape(block_keys, half_width)],
            axis=1,
        )
        grad_keyval = lax.dynamic_update_slice_in_dim(
            grad_keyval, merged, step_index * block_keys, 0
        )
        return (grad_query, grad_keyval)

    initial = (jnp.zeros(queries.shape, jnp.float32), jnp.zeros(gathered.shape, jnp.float32))
    return lax.fori_loop(0, block_count, back_visit_block, initial)


def per_device(
    tokens,
    attn_gain,
    mix_gain,
    query_key_value_weight,
    output_weight,
    router_weight,
    w_in,
    w_exp_out,
    out_grad,
    group_slot,
    group_routes,
    route_order,
):
    query_rows = tokens.shape[1]
    model_width = tokens.shape[2]
    head_count = HEADS
    head_size = model_width // head_count
    block_keys = math.gcd(query_rows, 512)
    first_query = lax.axis_index("context") * query_rows
    inputs = tokens[0].astype(jnp.float32)
    normed_one, inv_rms_one = norm_forward(inputs, attn_gain)
    act_low = normed_one.astype(jnp.bfloat16)
    qkv_low = jnp.dot(act_low, query_key_value_weight, preferred_element_type=jnp.float32).astype(
        jnp.bfloat16
    )
    queries = split_heads(qkv_low[:, :model_width], head_count)
    keyval = qkv_low[:, model_width:]
    initial = (
        jnp.full((head_count, query_rows), MASKED, jnp.float32),
        jnp.zeros((head_count, query_rows), jnp.float32),
        jnp.zeros((query_rows, head_count, head_size), jnp.float32),
    )
    fold_local = partial(fold_keys, queries=queries, first_query=first_query, block_keys=block_keys)
    run_peak, run_total, run_accum = fold_local(
        initial, lax.all_gather(keyval, "context", axis=0, tiled=True), jnp.int32(0)
    )
    attn_heads = run_accum / jnp.transpose(run_total)[:, :, None]
    log_total = run_peak + jnp.log(run_total)
    attention_reduced = attn_heads.reshape(query_rows, model_width).astype(jnp.bfloat16)
    residual = inputs + jnp.dot(
        attention_reduced, output_weight, preferred_element_type=jnp.float32
    )
    normed_two, inv_rms_two = norm_forward(residual, mix_gain)
    mixing_input = normed_two.astype(jnp.bfloat16)
    mixing_logits = jnp.dot(mixing_input, router_weight, preferred_element_type=jnp.float32)
    slot_row = group_slot[0]
    inverse = (
        jnp.zeros((query_rows,), jnp.int32)
        .at[slot_row]
        .set(jnp.arange(query_rows, dtype=jnp.int32))
    )
    groups, top_count = group_routes.shape
    experts = router_weight.shape[1]
    members = query_rows // groups
    capacity = 5 * groups * top_count // (4 * experts)
    local_experts = w_in.shape[0]
    sources = experts // local_experts
    slot_total = experts * capacity
    grouped_in = mixing_input[inverse].reshape(groups, members, model_width)
    grouped_logit = mixing_logits[inverse].reshape(groups, members, experts)
    route_index = jnp.broadcast_to(group_routes[:, None, :], (groups, members, top_count))
    chosen = jnp.take_along_axis(grouped_logit, route_index, axis=2)
    weights = jax.nn.softmax(chosen, axis=1)
    mix_low = weights.astype(jnp.bfloat16)
    mixed_rows = jnp.einsum(
        "gtk,gtd->gkd", mix_low, grouped_in, preferred_element_type=jnp.float32
    ).astype(jnp.bfloat16)
    pair_index = place_pairs(group_routes.reshape(-1), route_order.reshape(-1), capacity, experts)
    send_rows = (
        jnp.zeros((slot_total + 1, model_width), jnp.bfloat16)
        .at[pair_index]
        .set(mixed_rows.reshape(-1, model_width))
    )
    received = lax.all_to_all(
        send_rows[:slot_total].reshape(experts, capacity, model_width),
        "experts",
        split_axis=0,
        concat_axis=0,
        tiled=True,
    )
    received = received.reshape(sources, local_experts, capacity, model_width)
    pre_act = jnp.einsum("secd,edh->sech", received, w_in, preferred_element_type=jnp.float32)
    hidden_act, gate_pull = jax.vjp(smooth_gate, pre_act)
    hidden_low = hidden_act.astype(jnp.bfloat16)
    expert_res = jnp.einsum(
        "sech,ehd->secd", hidden_low, w_exp_out, preferred_element_type=jnp.float32
    ).astype(jnp.bfloat16)
    returned = lax.all_to_all(
        expert_res.reshape(experts, capacity, model_width),
        "experts",
        split_axis=0,
        concat_axis=0,
        tiled=True,
    )
    zero_row = jnp.zeros((1, model_width), jnp.bfloat16)
    outputs = jnp.concatenate([returned.reshape(slot_total, model_width), zero_row], axis=0)[
        pair_index
    ]
    outputs = outputs.reshape(groups, top_count, model_width)
    combined = jnp.einsum(
        "gtk,gkd->gtd", mix_low, outputs, preferred_element_type=jnp.float32
    ).reshape(query_rows, model_width)
    layer_out = (residual + combined[slot_row]).astype(jnp.bfloat16)
    grad_top = out_grad[0]
    grouped_grad = grad_top[inverse].reshape(groups, members, model_width)
    grad_w_comb = jnp.einsum(
        "gtd,gkd->gtk", grouped_grad, outputs, preferred_element_type=jnp.float32
    )
    grad_out_rows = jnp.einsum(
        "gtk,gtd->gkd", mix_low, grouped_grad, preferred_element_type=jnp.float32
    ).astype(jnp.bfloat16)
    grad_send = (
        jnp.zeros((slot_total + 1, model_width), jnp.bfloat16)
        .at[pair_index]
        .set(grad_out_rows.reshape(-1, model_width))
    )
    grad_recv = lax.all_to_all(
        grad_send[:slot_total].reshape(experts, capacity, model_width),
        "experts",
        split_axis=0,
        concat_axis=0,
        tiled=True,
    )
    grad_recv = grad_recv.reshape(sources, local_experts, capacity, model_width)
    w_exp_out_grad = jnp.einsum(
        "sech,secd->ehd", hidden_low, grad_recv, preferred_element_type=jnp.float32
    )
    grad_hidden = jnp.einsum(
        "secd,ehd->sech", grad_recv, w_exp_out, preferred_element_type=jnp.float32
    )
    grad_pre = gate_pull(grad_hidden)[0].astype(jnp.bfloat16)
    w_in_grad = jnp.einsum("secd,sech->edh", received, grad_pre, preferred_element_type=jnp.float32)
    grad_owner = jnp.einsum(
        "sech,edh->secd", grad_pre, w_in, preferred_element_type=jnp.float32
    ).astype(jnp.bfloat16)
    grad_back = lax.all_to_all(
        grad_owner.reshape(experts, capacity, model_width),
        "experts",
        split_axis=0,
        concat_axis=0,
        tiled=True,
    )
    grad_mixed = jnp.concatenate([grad_back.reshape(slot_total, model_width), zero_row], axis=0)[
        pair_index
    ]
    grad_mixed = grad_mixed.reshape(groups, top_count, model_width)
    grad_w_mix = jnp.einsum(
        "gkd,gtd->gtk", grad_mixed, grouped_in, preferred_element_type=jnp.float32
    )
    grad_members = jnp.einsum(
        "gtk,gkd->gtd", mix_low, grad_mixed, preferred_element_type=jnp.float32
    )
    grad_weights = grad_w_comb + grad_w_mix
    grad_chosen = weights * (grad_weights - jnp.sum(weights * grad_weights, axis=1, keepdims=True))
    route_onehot = (group_routes[:, :, None] == jnp.arange(experts)[None, None, :]).astype(
        jnp.float32
    )
    grad_grouped = jnp.einsum(
        "gtk,gke->gte", grad_chosen, route_onehot, precision=lax.Precision.HIGHEST
    ).astype(jnp.bfloat16)
    grad_logits = grad_grouped.reshape(query_rows, experts)[slot_row]
    route_grad = jnp.einsum(
        "td,te->de", mixing_input, grad_logits, preferred_element_type=jnp.float32
    )
    grad_mix = grad_members.reshape(query_rows, model_width)[slot_row] + jnp.einsum(
        "te,de->td", grad_logits, router_weight, preferred_element_type=jnp.float32
    )
    grad_norm_two, mix_gain_grad = norm_backward(residual, inv_rms_two, mix_gain, grad_mix)
    grad_residual = grad_top.astype(jnp.float32) + grad_norm_two
    grad_proj = grad_residual.astype(jnp.bfloat16)
    out_proj_grad = jnp.einsum(
        "td,te->de", attention_reduced, grad_proj, preferred_element_type=jnp.float32
    )
    grad_att = jnp.einsum(
        "te,de->td", grad_proj, output_weight, preferred_element_type=jnp.float32
    ).astype(jnp.bfloat16)
    grad_heads = split_heads(grad_att, head_count)
    delta_rows = jnp.transpose(jnp.sum(grad_heads.astype(jnp.float32) * attn_heads, axis=-1))
    keys_back = lax.all_gather(keyval, "context", axis=0, tiled=True)
    grad_query, grad_keyval = back_keys(
        keys_back, queries, grad_heads, delta_rows, log_total, first_query, block_keys
    )
    cycle_size = lax.axis_size("context")
    own_index = lax.axis_index("context")

    def take_block(block_id):
        return lax.dynamic_slice_in_dim(grad_keyval, block_id * query_rows, query_rows, 0)

    def pass_on(step_index, carried):
        moved = passed_along(carried.astype(jnp.bfloat16), "context", 1).astype(carried.dtype)
        block_id = (own_index - 2 - step_index + 2 * cycle_size) % cycle_size
        return moved + take_block(block_id)

    start_block = take_block((own_index - 1 + cycle_size) % cycle_size)
    own_keyval = lax.fori_loop(0, cycle_size - 1, pass_on, start_block)
    grad_qkv = jnp.concatenate(
        [grad_query.reshape(query_rows, model_width), own_keyval], axis=1
    ).astype(jnp.bfloat16)
    qkv_grad = jnp.einsum("td,te->de", act_low, grad_qkv, preferred_element_type=jnp.float32)
    grad_act = jnp.einsum(
        "te,de->td", grad_qkv, query_key_value_weight, preferred_element_type=jnp.float32
    )
    grad_norm_one, attn_gain_grad = norm_backward(inputs, inv_rms_one, attn_gain, grad_act)
    token_grad = grad_residual + grad_norm_one
    dense_sums = lax.psum(
        (attn_gain_grad, mix_gain_grad, qkv_grad, out_proj_grad, route_grad),
        ("experts", "context", "dp"),
    )
    expert_sums = (
        lax.psum(w_in_grad.astype(jnp.bfloat16), ("context", "dp")).astype(jnp.float32),
        lax.psum(w_exp_out_grad.astype(jnp.bfloat16), ("context", "dp")).astype(jnp.float32),
    )
    return (
        layer_out[None],
        token_grad[None],
        dense_sums[0],
        dense_sums[1],
        dense_sums[2],
        dense_sums[3],
        dense_sums[4],
        expert_sums[0],
        expert_sums[1],
    )


def solution(mesh):
    return jax.shard_map(
        per_device,
        mesh=mesh,
        in_specs=(
            P(("experts", "dp"), "context", None),
            P(),
            P(),
            P(),
            P(),
            P(),
            P("experts", None, None),
            P("experts", None, None),
            P(("experts", "dp"), "context", None),
            P(("experts", "dp"), "context"),
            P(("experts", "context", "dp"), None),
            P(("experts", "context", "dp"), None),
        ),
        out_specs=(
            P(("experts", "dp"), "context", None),
            P(("experts", "dp"), "context", None),
            P(),
            P(),
            P(),
            P(),
            P(),
            P("experts", None, None),
            P("experts", None, None),
        ),
        check_vma=False,
    )
```

profile of v0, /device:TPU:0, one launch (start us, length us, event | category | flops | bytes accessed | tf_op | source)
XLA Modules:
  0.0 1068.5 jit_solution(3388636967692149106)
XLA Ops:
  27.5 6.7 gather_fusion.4
  35.6 69.2 %all-gather.2.cloned.1.call-done = bf16[4096,1024]{1,0:T(8,128)(2,1)} async-done(((bf16[1024,1024]{1,0:T(8,128)(2,1)}), bf16[4096,1024]{1,0:T(8,128)(2,1)}) %all-gather.2.cloned.1.call-update) | async-done | bytes 8388624 | tf_op jit(solution)/shard_map/all_gather | solution.py:175
  104.8 11.9 %copy.195 = bf16[4096,1024]{0,1:T(8,128)(2,1)} copy(bf16[4096,1024]{1,0:T(8,128)(2,1)} %all-gather.2.cloned.1.call-done) | data formatting | bytes 16777216
  118.3 33.9 %while.44 = (s32[]{:T(128)}, f32[8,1024]{1,0:T(8,128)S(1)}, f32[8,1024]{1,0:T(8,128)S(1)}, f32[1024,8,64]{0,2,1:T(8,128)}, s32[]{:T(128)}, /*index=5*/bf16[4096,...) while((s32[]{:T(128)}, f32[8,1024]{1,0:T(8,128)S(1)}, ...), condition=%wide.region_4.5_spmd.clone, body=%wide.region_1.4_spmd.clone.sunk | while | flops 1129866752 | bytes 78131464 | solution.py:85
  164.0 34.4 %gather_fusion.8 = f32[4096]{0:T(1024)S(1)} fusion(f32[32,32,8]{2,1,0:T(8,128)S(1)} %bitcast.226, s32[4096]{0:T(1024)S(1)} %reshape.372), kind=kCustom, calls=%fused_computation.8 | custom fusion | bytes 81920 | tf_op jit(solution)/shard_map/jit(take_along_axis)/gather | solution.py:202
  265.1 6.9 gather_fusion.6
  284.3 6.9 gather_fusion.3
  302.1 7.9 broadcast_in_dim.113
  310.0 85.7 %while.45 = (s32[]{:T(128)}, f32[1024,8,64]{0,2,1:T(8,128)}, f32[4096,1024]{0,1:T(8,128)}, s32[]{:T(128)}, bf16[4096,1024]{0,1:T(8,128)(2,1)}, /*index=5*/bf16[1...) while((s32[]{:T(128)}, f32[1024,8,64]{0,2,1:T(8,128)}, ...), condition=%wide.region_16.17_spmd.clone, body=%wide.region_15.16_spmd.clone.sunk | while | flops 2728658432 | bytes 154251664 | solution.py:137
  311.5 8.1 fusion.196
  320.0 9.3 fusion.197
  334.1 10.3 fusion.198
  353.3 8.8 fusion.196
  362.5 9.5 fusion.197
  376.7 11.0 %fusion.198 = f32[8,512,64]{1,2,0:T(8,128)} fusion(bf16[1024,8,64]{0,2,1:T(8,128)(2,1)} %get-tuple-element.733, f32[8,512,1024]{2,1,0:T(8,128)} %fusion.196, f32[8,1024]{1,0:T(8,128)S(1)} %get-tuple-element.732, pred[1024,512]{0,1:T(8,128)(4,1)S(1)} %broadcast_compare_fusion.6), kind=kOutput, calls=%fused_computation.38.clone.1 | convolution fusion | flops 553648128 | bytes 19431424 | tf_op jit(solution)/shard_map/while/body/hqk,qhd->khd/dot_general | solution.py:108
  387.7 6.2 convolution_multiply_fusion.2
  412.2 498.3 %while.43 = (s32[]{:T(128)}, bf16[1024,1024]{1,0:T(8,128)(2,1)}, s32[]{:T(128)}, f32[4096,1024]{0,1:T(8,128)}, s32[]{:T(128)}, /*index=5*/s32[]{:T(128)}, s32[]{...) while((s32[]{:T(128)}, bf16[1024,1024]{1,0:T(8,128)(2,1)}, s32[]{:T(128)}, ...), condition=%wide.region_18.19_spmd, body=%wide.region_17.18_spmd.sunk | while | flops 3145747 | bytes 33554764 | solution.py:335
  412.2 120.2 %collective-permute-start = (bf16[1024,1024]{1,0:T(8,128)(2,1)}, bf16[1024,1024]{1,0:T(8,128)(2,1)}, u32[]{:S(2)}, u32[]{:S(2)}) collective-permute-start(bf16[1024,1024]{1,0:T(8,128)(2,1)} %get-tuple-element.753), channel_id=1, source_target_pairs={{6,0},{0,2},{2,4},{4,6},{7,1},{1,3},{3,5},{5,7},{14,8},{8,10},{10,... | collective-permute-start | bytes 6291464 | tf_op jit(solution)/shard_map/while/body/eval_jaxpr/ppermute | solution.py:19
  542.5 265.4 %collective-permute-done = bf16[1024,1024]{1,0:T(8,128)(2,1)} collective-permute-done((bf16[1024,1024]{1,0:T(8,128)(2,1)}, bf16[1024,1024]{1,0:T(8,128)(2,1)}, u32[]{:S(2)}, u32[]{:S(2)}) %collective-permute-start) | collective-permute-done | bytes 2097184 | tf_op jit(solution)/shard_map/while/body/eval_jaxpr/ppermute | solution.py:19
  823.0 34.2 %collective-permute-done = bf16[1024,1024]{1,0:T(8,128)(2,1)} collective-permute-done((bf16[1024,1024]{1,0:T(8,128)(2,1)}, bf16[1024,1024]{1,0:T(8,128)(2,1)}, u32[]{:S(2)}, u32[]{:S(2)}) %collective-permute-start) | collective-permute-done | bytes 2097184 | tf_op jit(solution)/shard_map/while/body/eval_jaxpr/ppermute | solution.py:19
  872.3 33.3 %collective-permute-done = bf16[1024,1024]{1,0:T(8,128)(2,1)} collective-permute-done((bf16[1024,1024]{1,0:T(8,128)(2,1)}, bf16[1024,1024]{1,0:T(8,128)(2,1)}, u32[]{:S(2)}, u32[]{:S(2)}) %collective-permute-start) | collective-permute-done | bytes 2097184 | tf_op jit(solution)/shard_map/while/body/eval_jaxpr/ppermute | solution.py:19
  927.5 40.0 %all-reduce.2 = (f32[512]{0:T(512)}, f32[512]{0:T(512)}, f32[512,8]{0,1:T(8,128)}) all-reduce(f32[512]{0:T(512)S(1)} %get-tuple-element.429, f32[512]{0:T(512)S(1)} %copy-done.56, f32[512,8]{0,1:T(8,128)S(1)} %fusion.116), channel_id=1, replica_groups=mesh['experts'=4,'context'=4,'dp'=2] {'experts','context','dp'}, use_global_device_ids=true, to_apply=%region_21.22 | all-reduce | flops 5120 | bytes 40960 | tf_op jit(solution)/shard_map/psum | solution.py:345
  967.6 6.8 convert_element_type.136
  979.0 77.8 %all-reduce.8.cloned.1.call-done = (f32[512,1536]{1,0:T(8,128)}, f32[512,512]{1,0:T(8,128)}) async-done(((f32[512,1536]{1,0:T(8,128)}, f32[512,512]{1,0:T(8,128)}), (f32[512,1536]{1,0:T(8,128)}, f32[512,512]{1,0:T(8,128)})) %all-reduce.8.cloned.1.call-update) | async-done | bytes 4194320 | tf_op jit(solution)/shard_map/psum | solution.py:345
  (301 shorter events, 267.8 us)
Async XLA Ops:
  7.2 97.6 %all-gather.2.cloned.1.call-start = ((), (), s32[]{:S(2)}) async-start(), calls=%async_computation.4 | async-start | bytes 10485760 | tf_op jit(solution)/shard_map/all_gather | solution.py:175
  18.3 16.0 %copy-start.43 = (s32[32,4]{1,0:T(8,128)}, s32[32,4]{1,0:T(8,128)S(1)}, u32[]{:S(2)}) copy-start(s32[32,4]{1,0:T(8,128)S(1)} %copy.198) | copy-start | bytes 1540
  27.5 133.6 %copy-start.45 = (s32[1024]{0:T(1024)}, s32[1024]{0:T(1024)S(1)}, u32[]{:S(2)}) copy-start(s32[1024]{0:T(1024)S(1)} %fusion.96) | copy-start | bytes 12292
  34.4 82.3 %copy-start.62 = (s32[128]{0:T(128)}, s32[128]{0:T(128)S(1)}, u32[]{:S(2)}) copy-start(s32[128]{0:T(128)S(1)} %fusion.101) | copy-start | bytes 1540
  164.0 35.2 %copy-start.46 = (s32[1024]{0:T(1024)S(1)}, s32[1024]{0:T(1024)}, u32[]{:S(2)}) copy-start(s32[1024]{0:T(1024)} %copy-done.45) | copy-start | bytes 12292
  204.6 9.5 copy-start.20
  207.5 8.8 copy-start.26
  207.5 8.8 copy-start.32
  209.5 12.1 %all-to-all-start = ((bf16[8,20,512]{2,1,0:T(8,128)(2,1)}), bf16[8,20,512]{2,1,0:T(8,128)(2,1)S(1)}, u32[]{:S(2)}, u32[]{:S(2)}) async-start(bf16[8,20,512]{2,1,0:T(8,128)(2,1)} %reshape.290), calls=%async_computation | async-start | bytes 393216 | tf_op jit(solution)/shard_map/all_to_all | solution.py:214
  221.6 9.6 all-to-all-start.2
  241.9 10.5 all-to-all-start.1
  246.2 721.4 %all-reduce.10.cloned.1.call-start = ((), (), s32[]{:S(2)}) async-start(), calls=%async_computation.6 | async-start | bytes 16777216 | tf_op jit(solution)/shard_map/psum | solution.py:350
  252.4 9.8 all-to-all-start.3
  255.9 800.8 %all-reduce.8.cloned.1.call-start = ((), (), s32[]{:S(2)}) async-start(), calls=%async_computation.5 | async-start | bytes 8388608 | tf_op jit(solution)/shard_map/psum | solution.py:345
  311.5 8.5 copy-start.38
  320.0 9.3 copy-start.4
  353.3 9.2 copy-start.38
  362.5 9.5 copy-start.4
  412.2 498.3 %copy-start.17 = (bf16[1,1024,512]{1,2,0:T(8,128)(2,1)S(1)}, bf16[1,1024,512]{1,2,0:T(8,128)(2,1)}, u32[]{:S(2)}) copy-start(bf16[1,1024,512]{1,2,0:T(8,128)(2,1)} %copy-done.15) | copy-start | bytes 3145732
  412.2 498.3 %copy-start.54 = (f32[1024]{0:T(1024)S(1)}, f32[1024]{0:T(1024)}, u32[]{:S(2)}) copy-start(f32[1024]{0:T(1024)} %copy-done.53) | copy-start | bytes 12292
  412.2 498.3 %copy-start.60 = (f32[512]{0:T(512)S(1)}, f32[512]{0:T(512)}, u32[]{:S(2)}) copy-start(f32[512]{0:T(512)} %param.19) | copy-start | bytes 6148
  412.2 395.7 %collective-permute-start = (bf16[1024,1024]{1,0:T(8,128)(2,1)}, bf16[1024,1024]{1,0:T(8,128)(2,1)}, u32[]{:S(2)}, u32[]{:S(2)}) collective-permute-start(bf16[1024,1024]{1,0:T(8,128)(2,1)} %get-tuple-element.753), channel_id=1, source_target_pairs={{6,0},{0,2},{2,4},{4,6},{7,1},{1,3},{3,5},{5,7},{14,8},{8,10},{10,... | collective-permute-start | bytes 6291464 | tf_op jit(solution)/shard_map/while/body/eval_jaxpr/ppermute | solution.py:19
  812.8 44.3 %collective-permute-start = (bf16[1024,1024]{1,0:T(8,128)(2,1)}, bf16[1024,1024]{1,0:T(8,128)(2,1)}, u32[]{:S(2)}, u32[]{:S(2)}) collective-permute-start(bf16[1024,1024]{1,0:T(8,128)(2,1)} %get-tuple-element.753), channel_id=1, source_target_pairs={{6,0},{0,2},{2,4},{4,6},{7,1},{1,3},{3,5},{5,7},{14,8},{8,10},{10,... | collective-permute-start | bytes 6291464 | tf_op jit(solution)/shard_map/while/body/eval_jaxpr/ppermute | solution.py:19
  862.1 43.4 %collective-permute-start = (bf16[1024,1024]{1,0:T(8,128)(2,1)}, bf16[1024,1024]{1,0:T(8,128)(2,1)}, u32[]{:S(2)}, u32[]{:S(2)}) collective-permute-start(bf16[1024,1024]{1,0:T(8,128)(2,1)} %get-tuple-element.753), channel_id=1, source_target_pairs={{6,0},{0,2},{2,4},{4,6},{7,1},{1,3},{3,5},{5,7},{14,8},{8,10},{10,... | collective-permute-start | bytes 6291464 | tf_op jit(solution)/shard_map/while/body/eval_jaxpr/ppermute | solution.py:19
  (57 other events, 193.7 us)
Sparse Core Ops, SparseCore 0:
  14.5 90.2 all-gather.1
  250.9 227.8 all-reduce.9
  916.0 140.6 all-reduce.7
where the time goes:
time: 1080 us; the launch traced here: 1070 us
  waiting for transfers between devices  490 us (45%)
  local copies, waits for them, and re-layouts  192 us (18%)
  matrix products  139 us (13%)
  starting transfers between devices  136 us (13%)
  other arithmetic  54.6 us (5%)
  blocking collectives  40 us (4%)
  between operations  14.9 us (1%)
    ppermute x3, waiting for transfers between devices, passed_along(): return lax.ppermute(block, axis, route)  333 us
    ppermute x3, starting transfers between devices, passed_along(): return lax.ppermute(block, axis, route)  120 us
    psum x1, waiting for transfers between devices, per_device(): lax.psum((attn_gain_grad, mix_gain_grad, qkv_grad, out_proj_grad, route_g...  77.8 us
    all_gather x1, waiting for transfers between devices, per_device(): lax.all_gather(keyval, 'context', axis=0, tiled=True)  69.2 us
    psum x1, blocking collectives, per_device(): lax.psum((attn_gain_grad, mix_gain_grad, qkv_grad, out_proj_grad, route_g...  40 us
    gather x5, local copies, waits for them, and re-layouts, per_device(): chosen = jnp.take_along_axis(grouped_logit, route_index, axis=2)  35.7 us
    dynamic_slice x7, local copies, waits for them, and re-layouts, take_block(): lax.dynamic_slice_in_dim(grad_keyval, block_id * query_rows, query_rows, 0)  34.2 us
    unnamed x123, local copies, waits for them, and re-layouts  31.9 us
  transfers between devices with their start and end apart: 10, of which 9 were waited for; matrix products, arithmetic and copies ran while one was open for 24% of the time, Pallas kernels for 0%

commit v1 on v0

v1 whole, which is shorter than its diff:
```python
import functools

import jax
import jax.numpy as jnp
import numpy as np
from jax import lax
from jax.experimental import pallas as pl
from jax.experimental.pallas import tpu as pltpu
from jax.sharding import PartitionSpec as P

HEADS = 8
NORM_EPS = 1e-05
MASKED = -1e30
F32 = jnp.float32
BF = jnp.bfloat16
MESH = pl.DeviceIdType.MESH
VMEM = pl.BlockSpec(memory_space=pltpu.VMEM)
ANY = pl.BlockSpec(memory_space=pl.ANY)
LIMIT = 60 << 20
TILE = 512


def dotf(a, b, dims=((1,), (0,)), **kw):
    return lax.dot_general(a, b, (dims, ((), ())), preferred_element_type=F32, **kw)


def params(**kw):
    return pltpu.CompilerParams(vmem_limit_bytes=LIMIT, **kw)


def sequence_of(c):
    return lax.rem(lax.rem(c, 2) + c // 2, 2)


def chip_of(seq, rank):
    return 2 * rank + lax.rem(seq + rank, 2)


def coords():
    return lax.axis_index("context"), lax.axis_index("dp")


def plane_barrier(c, d):
    barrier = pltpu.get_barrier_semaphore()
    for k in range(1, 8):
        other = lax.rem(2 * c + d + k, 8)
        pl.semaphore_signal(
            barrier,
            inc=1,
            device_id={"context": other // 2, "dp": lax.rem(other, 2)},
            device_id_type=MESH,
        )
    pl.semaphore_wait(barrier, 7)


def remote(src, dst, send_sem, recv_sem, context, dp):
    return pltpu.make_async_remote_copy(
        src_ref=src,
        dst_ref=dst,
        send_sem=send_sem,
        recv_sem=recv_sem,
        device_id={"context": context, "dp": dp},
        device_id_type=MESH,
    )


def gather_kernel(x_ref, g_ref, local, full_s, full_r, s1, s2, hr, fs, fr):
    c, d = coords()
    seq = sequence_of(c)
    half = x_ref.shape[0] // 2
    plane_barrier(c, d)
    native = d == seq
    far = 3 - c
    side = 2 * (c // 2) + 1 - lax.rem(c, 2)
    over = 2 * (1 - c // 2) + lax.rem(c, 2)

    def part(ref, e):
        return ref.at[pl.ds(e * half, half)]

    def send(target, e, sem, slot):
        return remote(part(x_ref, e), part(g_ref.at[c], e), sem.at[e], hr.at[slot], target, e)

    @pl.when(native)
    def _():
        for e in range(2):
            send(far, e, s1, 0).start()
        remote(x_ref, g_ref.at[c], full_s, full_r, c, 1 - d).start()
        pltpu.make_async_copy(x_ref, g_ref.at[c], local).start()

    @pl.when(jnp.logical_not(native))
    def _():
        for e in range(2):
            send(side, e, s1, 1).start()
            send(over, e, s2, 2).start()

    forward = []
    for slot, source in ((1, side), (2, over), (0, far)):
        mine = part(g_ref.at[source], d)
        remote(mine, mine, s1.at[0], hr.at[slot], c, d).wait_recv()
        copy = remote(mine, mine, fs.at[slot], fr.at[slot], c, 1 - d)
        copy.start()
        forward.append(copy)

    @pl.when(native)
    def _():
        for e in range(2):
            send(far, e, s1, 0).wait_send()
        remote(x_ref, g_ref.at[c], full_s, full_r, c, 1 - d).wait_send()
        pltpu.make_async_copy(x_ref, g_ref.at[c], local).wait()

    @pl.when(jnp.logical_not(native))
    def _():
        for e in range(2):
            send(side, e, s1, 1).wait_send()
            send(over, e, s2, 2).wait_send()
        remote(x_ref, g_ref.at[c], full_s, full_r, c, 1 - d).wait_recv()

    for copy in forward:
        copy.wait_send()
    for slot, source in ((1, side), (2, over), (0, far)):
        theirs = part(g_ref.at[source], 1 - d)
        remote(theirs, theirs, fs.at[slot], fr.at[slot], c, 1 - d).wait_recv()


def gather_tokens(x, context):
    return pl.pallas_call(
        gather_kernel,
        out_shape=jax.ShapeDtypeStruct((context,) + x.shape, x.dtype),
        in_specs=[ANY],
        out_specs=ANY,
        scratch_shapes=[
            pltpu.SemaphoreType.DMA,
            pltpu.SemaphoreType.DMA,
            pltpu.SemaphoreType.DMA,
            pltpu.SemaphoreType.DMA((2,)),
            pltpu.SemaphoreType.DMA((2,)),
            pltpu.SemaphoreType.DMA((3,)),
            pltpu.SemaphoreType.DMA((3,)),
            pltpu.SemaphoreType.DMA((3,)),
        ],
        compiler_params=params(collective_id=0, has_side_effects=True),
    )(x)


def home_kernel(x_ref, o_ref, local, send, recv):
    c, e = coords()
    seq = sequence_of(c)
    pair = 2 * (c // 2) + e
    plane_barrier(c, e)
    for k in range(4):
        b = lax.rem(c + 3 - k, 4)
        own = jnp.logical_and(b == c, e == seq)

        @pl.when(own)
        def _():
            pltpu.make_async_copy(x_ref.at[b], o_ref.at[pair], local).start()

        @pl.when(jnp.logical_not(own))
        def _():
            remote(x_ref.at[b], o_ref.at[pair], send.at[b], recv.at[pair], b, seq).start()

    for b in range(4):
        own = jnp.logical_and(b == c, e == seq)

        @pl.when(own)
        def _():
            pltpu.make_async_copy(x_ref.at[b], o_ref.at[pair], local).wait()

        @pl.when(jnp.logical_not(own))
        def _():
            remote(x_ref.at[b], o_ref.at[pair], send.at[b], recv.at[pair], b, seq).wait_send()

    for h in range(4):
        own = jnp.logical_and(h == pair, e == seq)

        @pl.when(jnp.logical_not(own))
        def _():
            remote(x_ref.at[h], o_ref.at[h], send.at[h], recv.at[h], c, e).wait_recv()


def to_home(x, cid):
    return pl.pallas_call(
        home_kernel,
        out_shape=jax.ShapeDtypeStruct(x.shape, x.dtype),
        in_specs=[ANY],
        out_specs=ANY,
        scratch_shapes=[
            pltpu.SemaphoreType.DMA,
            pltpu.SemaphoreType.DMA((4,)),
            pltpu.SemaphoreType.DMA((4,)),
        ],
        compiler_params=params(collective_id=cid, has_side_effects=True),
    )(x)


def heads_kernel(x_ref, o_ref, local, send, recv):
    c, d = coords()
    seq = sequence_of(c)
    plane_barrier(c, d)
    for h in range(4):
        chip = chip_of(d, h // 2)
        e = h % 2
        own = jnp.logical_and(chip == c, e == d)

        @pl.when(own)
        def _():
            pltpu.make_async_copy(x_ref.at[h], o_ref.at[c], local).start()

        @pl.when(jnp.logical_not(own))
        def _():
            remote(x_ref.at[h], o_ref.at[c], send.at[h], recv.at[c], chip, e).start()

    for h in range(4):
        chip = chip_of(d, h // 2)
        e = h % 2
        own = jnp.logical_and(chip == c, e == d)

        @pl.when(own)
        def _():
            pltpu.make_async_copy(x_ref.at[h], o_ref.at[c], local).wait()

        @pl.when(jnp.logical_not(own))
        def _():
            remote(x_ref.at[h], o_ref.at[c], send.at[h], recv.at[c], chip, e).wait_send()

    for b in range(4):
        own = jnp.logical_and(b == c, d == seq)

        @pl.when(jnp.logical_not(own))
        def _():
            remote(x_ref.at[b], o_ref.at[b], send.at[b], recv.at[b], c, d).wait_recv()


def to_heads(x, cid):
    return pl.pallas_call(
        heads_kernel,
        out_shape=jax.ShapeDtypeStruct(x.shape, x.dtype),
        in_specs=[ANY],
        out_specs=ANY,
        scratch_shapes=[
            pltpu.SemaphoreType.DMA,
            pltpu.SemaphoreType.DMA((4,)),
            pltpu.SemaphoreType.DMA((4,)),
        ],
        compiler_params=params(collective_id=cid, has_side_effects=True),
    )(x)


def attention_kernel(x_ref, gain_ref, w_ref, qkv_ref, o_ref, lse_ref, ws, vx, acc):
    length = x_ref.shape[0]
    tq, tk = 1024, 512
    c, e = coords()
    pair = 2 * (c // 2) + e
    lane = lax.broadcasted_iota(jnp.int32, (1, 128), 1)
    low = lane < 64
    width = w_ref.shape[0]
    for i in range(3):
        ws[:, 128 * i : 128 * i + 128] = w_ref[
            :, pl.ds(pl.multiple_of(i * width + pair * 128, 128), 128)
        ]

    @pl.loop(0, length // TILE)
    def _(t):
        rows = pl.ds(pl.multiple_of(t * TILE, TILE), TILE)
        x = x_ref[rows, :].astype(F32)
        inv = lax.rsqrt(jnp.mean(x * x, axis=1, keepdims=True) + NORM_EPS)
        act = (x * inv * gain_ref[...]).astype(BF)
        qkv = dotf(act, ws[...]).astype(BF)
        qkv_ref[rows, 0:128] = qkv[:, 0:128] * jnp.asarray(0.125, BF)
        qkv_ref[rows, 128:384] = qkv[:, 128:384]
        vt = jnp.transpose(qkv[:, 256:384].astype(F32)).astype(BF)
        for h in range(2):
            vx[h, 0:64, rows] = vt[64 * h : 64 * h + 64, :]
            vx[h, 64:80, rows] = jnp.ones((16, TILE), BF)

    def step(i, j, qs, carry, diag):
        krows = pl.ds(pl.multiple_of(j * tk, tk), tk)
        k = qkv_ref[krows, 128:256]
        out = []
        first = 0 if diag is None else diag * tk
        cols = slice(first, tq)
        for h in range(2):
            m = carry[h][:, cols]
            s = dotf(k, qs[h][cols, :], ((1,), (1,)))
            if diag is not None:
                kpos = lax.broadcasted_iota(jnp.int32, s.shape, 0)
                qpos = lax.broadcasted_iota(jnp.int32, s.shape, 1)
                s = jnp.where(kpos <= qpos, s, MASKED)
            mn = jnp.maximum(m, jnp.max(s, axis=0, keepdims=True))
            p = jnp.exp(s - mn).astype(BF)
            al = jnp.exp(m - mn)
            acc[h, :, cols] = acc[h, :, cols] * al + dotf(vx[h, :, krows], p)
            if first:
                mn = jnp.concatenate([carry[h][:, :first], mn], axis=1)
            out.append(mn)
        return tuple(out)

    @pl.loop(0, length // tq)
    def _(i):
        rows = pl.ds(pl.multiple_of(i * tq, tq), tq)
        q = qkv_ref[rows, 0:128]
        z = jnp.zeros_like(q)
        qs = [jnp.where(low, q, z), jnp.where(low, z, q)]
        acc[...] = jnp.zeros_like(acc)
        m0 = jnp.full((1, tq), MASKED, F32)
        carry = lax.fori_loop(0, i * (tq // tk), lambda j, m: step(i, j, qs, m, None), (m0, m0))
        for t in range(tq // tk):
            carry = step(i, i * (tq // tk) + t, qs, carry, t)
        parts = []
        for h in range(2):
            total = acc[h, 64:65, :]
            parts.append(acc[h, 0:64, :] / total)
            lse_ref[h : h + 1, rows] = carry[h] + jnp.log(total)
        o_ref[rows, :] = jnp.transpose(jnp.concatenate(parts, axis=0)).astype(BF)


def attention(x, gain, w):
    length = x.shape[0]
    return pl.pallas_call(
        attention_kernel,
        out_shape=(
            jax.ShapeDtypeStruct((length, 384), BF),
            jax.ShapeDtypeStruct((length, 128), BF),
            jax.ShapeDtypeStruct((2, length), F32),
        ),
        in_specs=[VMEM] * 3,
        out_specs=(VMEM,) * 3,
        scratch_shapes=[
            pltpu.VMEM((w.shape[0], 384), BF),
            pltpu.VMEM((2, 80, length), BF),
            pltpu.VMEM((2, 80, 1024), F32),
        ],
        compiler_params=params(),
        name="attention",
    )(x, gain, w)


def attention_back_kernel(qkv_ref, do_ref, o_ref, lse_ref, d_ref, qh, dh, kh, dq, delta):
    length = qkv_ref.shape[0]
    tq = tk = TILE
    low = lax.broadcasted_iota(jnp.int32, (1, 128), 1) < 64
    low_rows = lax.broadcasted_iota(jnp.int32, (128, 1), 0) < 64
    head_sum = (
        lax.broadcasted_iota(jnp.int32, (8, 128), 1) // 64
        == lax.broadcasted_iota(jnp.int32, (8, 128), 0)
    ).astype(F32)

    @pl.loop(0, length // TILE)
    def _(t):
        rows = pl.ds(pl.multiple_of(t * TILE, TILE), TILE)
        q = qkv_ref[rows, 0:128]
        g = do_ref[rows, :]
        z = jnp.zeros_like(q)
        qh[0, rows, :] = jnp.where(low, q, z)
        qh[1, rows, :] = jnp.where(low, z, q)
        dh[0, rows, :] = jnp.where(low, g, z)
        dh[1, rows, :] = jnp.where(low, z, g)
        kt = jnp.transpose(qkv_ref[rows, 128:256].astype(F32)).astype(BF)
        zt = jnp.zeros_like(kt)
        kh[0, :, rows] = jnp.where(low_rows, kt, zt)
        kh[1, :, rows] = jnp.where(low_rows, zt, kt)
        product = g.astype(F32) * o_ref[rows, :].astype(F32)
        delta[:, rows] = dotf(
            head_sum, product, ((1,), (1,)), precision=lax.Precision.HIGHEST
        )
        dq[:, rows] = jnp.zeros((128, TILE), F32)

    def step(i, j, k, v, masked):
        qrows = pl.ds(pl.multiple_of(i * tq, tq), tq)
        krows = pl.ds(pl.multiple_of(j * tk, tk), tk)
        dk = dv = dqt = 0.0
        for h in range(2):
            s = dotf(k, qh[h, qrows, :], ((1,), (1,)))
            p = jnp.exp(s - lse_ref[h : h + 1, qrows])
            if masked:
                kpos = lax.broadcasted_iota(jnp.int32, (tk, tq), 0)
                qpos = lax.broadcasted_iota(jnp.int32, (tk, tq), 1)
                p = jnp.where(kpos <= qpos, p, 0.0)
            dp = dotf(v, dh[h, qrows, :], ((1,), (1,)))
            ds = (p * (dp - delta[h : h + 1, qrows])).astype(BF)
            dv = dv + dotf(p.astype(BF), dh[h, qrows, :])
            dk = dk + dotf(ds, qh[h, qrows, :])
            dqt = dqt + dotf(kh[h, :, krows], ds)
        dq[:, qrows] = dq[:, qrows] + dqt
        return dk, dv

    @pl.loop(0, length // tk)
    def _(j):
        krows = pl.ds(pl.multiple_of(j * tk, tk), tk)
        k = qkv_ref[krows, 128:256]
        v = qkv_ref[krows, 256:384]
        first = step(j, j, k, v, True)

        def body(i, carry):
            dk, dv = step(i, j, k, v, False)
            return carry[0] + dk, carry[1] + dv

        dk, dv = lax.fori_loop(j + 1, length // tq, body, first)
        d_ref[krows, 128:256] = dk.astype(BF)
        d_ref[krows, 256:384] = dv.astype(BF)

    @pl.loop(0, length // TILE)
    def _(t):
        rows = pl.ds(pl.multiple_of(t * TILE, TILE), TILE)
        d_ref[rows, 0:128] = (jnp.transpose(dq[:, rows]) * 0.125).astype(BF)


def attention_back(qkv, do, o, lse):
    length = qkv.shape[0]
    return pl.pallas_call(
        attention_back_kernel,
        out_shape=jax.ShapeDtypeStruct((length, 384), BF),
        in_specs=[VMEM] * 4,
        out_specs=VMEM,
        scratch_shapes=[
            pltpu.VMEM((2, length, 128), BF),
            pltpu.VMEM((2, length, 128), BF),
            pltpu.VMEM((2, 128, length), BF),
            pltpu.VMEM((128, length), F32),
            pltpu.VMEM((8, length), F32),
        ],
        compiler_params=params(),
        name="attention_back",
    )(qkv, do, o, lse)


def mix_kernel(
    stride, capacity, local, choices,
    x_ref, att_ref, wo_ref, gain_ref, router_ref, slot_ref, pair_ref, gout_ref,
    res_ref, mix_ref, wts_ref, place_ref, send_ref,
    att,
):
    tokens = x_ref.shape[0]
    pairs = pair_ref.shape[1]
    experts = router_ref.shape[1]
    members = tokens * choices // pairs
    for h in range(4):
        att[:, 128 * h : 128 * h + 128] = att_ref[h]

    @pl.loop(0, tokens // 256)
    def _(t):
        rows = pl.ds(pl.multiple_of(t * 256, 256), 256)
        res = x_ref[rows, :].astype(F32) + dotf(att[rows, :], wo_ref[...])
        inv = lax.rsqrt(jnp.mean(res * res, axis=1, keepdims=True) + NORM_EPS)
        res_ref[rows, :] = res
        mix_ref[rows, :] = (res * inv * gain_ref[...]).astype(BF)

    routes = pair_ref[0:1, :]
    order = pair_ref[1:2, :]
    eye = lax.broadcasted_iota(jnp.int32, (pairs, pairs), 0) == lax.broadcasted_iota(
        jnp.int32, (pairs, pairs), 1
    )
    zero = jnp.zeros((pairs, pairs), F32)

    def as_column(row):
        return jnp.sum(jnp.where(eye, row.astype(F32), zero), axis=1, keepdims=True)

    route_col = as_column(routes)
    order_col = as_column(order)
    ahead = jnp.logical_and(route_col == routes.astype(F32), order_col < order.astype(F32))
    rank = jnp.sum(ahead.astype(F32), axis=0, keepdims=True).astype(jnp.int32)
    slots = place_ref.shape[0]
    block = lax.div(routes, local)
    place = block * stride + (routes - block * local) * capacity + rank
    place = jnp.where(rank < capacity, place, slots)
    spread = (lax.broadcasted_iota(jnp.int32, (slots, pairs), 0) == place).astype(BF)
    place_ref[...] = spread

    pick = (lax.broadcasted_iota(jnp.int32, (experts, pairs), 0) == routes).astype(F32)
    columns = dotf(router_ref[...].astype(F32), pick).astype(BF)
    chosen = dotf(columns, mix_ref[...], ((0,), (1,)))
    group = lax.broadcasted_iota(jnp.int32, (pairs, 1), 0) // choices
    member = group == slot_ref[...] // members
    chosen = jnp.where(member, chosen, MASKED)
    peak = jnp.max(chosen, axis=1, keepdims=True)
    weight = jnp.where(member, jnp.exp(chosen - peak), 0.0)
    weight = weight / jnp.sum(weight, axis=1, keepdims=True)
    wts_ref[...] = weight
    low = weight.astype(BF)
    width = mix_ref.shape[1]
    mixed = dotf(low, mix_ref[...]).astype(BF)
    send_ref[:, 0:width] = dotf(spread, mixed).astype(BF)
    dy = dotf(low, gout_ref[...]).astype(BF)
    send_ref[:, width:] = dotf(spread, dy).astype(BF)


def gelu_parts(x):
    scale = np.float32(np.sqrt(2.0 / np.pi))
    square = x * x
    t = jnp.tanh(scale * (x + np.float32(0.044715) * (square * x)))
    half = 0.5 * (1.0 + t)
    slope = half + (0.5 * x) * (1.0 - t * t) * (
        scale * (1.0 + np.float32(3 * 0.044715) * square)
    )
    return x * half, slope


def expert_kernel(steps, recv_ref, pick_ref, win_ref, wout_ref, rows_ref, ret_ref, y, dx):
    e = pl.program_id(0)
    f = pl.program_id(1)
    width = win_ref.shape[1]

    @pl.when(f == 0)
    def _():
        rows_ref[0] = dotf(pick_ref[0], recv_ref[...]).astype(BF)
        y[...] = jnp.zeros_like(y)
        dx[...] = jnp.zeros_like(dx)

    @pl.when(jnp.logical_and(e == 0, f == 0))
    def _():
        ret_ref[...] = jnp.zeros_like(ret_ref)

    x = rows_ref[0, :, 0:width]
    dy = rows_ref[0, :, width:]
    hidden, slope = gelu_parts(dotf(x, win_ref[0]))
    y[...] += dotf(hidden.astype(BF), wout_ref[0])
    d_pre = (dotf(dy, wout_ref[0], ((1,), (1,))) * slope).astype(BF)
    dx[...] += dotf(d_pre, win_ref[0], ((1,), (1,)))

    @pl.when(f == steps - 1)
    def _():
        both = jnp.concatenate([y[...].astype(BF), dx[...].astype(BF)], axis=1)
        ret_ref[...] += dotf(pick_ref[0], both, ((0,), (0,))).astype(BF)


def expert_rows(recv, pick, w_in, w_out):
    local, count, total = pick.shape
    _, width, hidden = w_in.shape
    chunk = 512
    steps = hidden // chunk
    return pl.pallas_call(
        functools.partial(expert_kernel, steps),
        grid=(local, steps),
        out_shape=(
            jax.ShapeDtypeStruct((local, count, 2 * width), BF),
            jax.ShapeDtypeStruct((total, 2 * width), BF),
        ),
        in_specs=[
            pl.BlockSpec((total, 2 * width), lambda e, f: (0, 0)),
            pl.BlockSpec((1, count, total), lambda e, f: (e, 0, 0)),
            pl.BlockSpec((1, width, chunk), lambda e, f: (e, 0, f)),
            pl.BlockSpec((1, chunk, width), lambda e, f: (e, f, 0)),
        ],
        out_specs=(
            pl.BlockSpec((1, count, 2 * width), lambda e, f: (e, 0, 0)),
            pl.BlockSpec((total, 2 * width), lambda e, f: (0, 0)),
        ),
        scratch_shapes=[pltpu.VMEM((count, width), F32), pltpu.VMEM((count, width), F32)],
        compiler_params=params(),
        name="expert_rows",
    )(recv, pick, w_in, w_out)


def expert_grad_kernel(rows_ref, win_ref, wout_ref, gin_ref, gout_ref, x, dy):
    width = win_ref.shape[1]
    copies, _, count, _ = rows_ref.shape

    @pl.when(pl.program_id(1) == 0)
    def _():
        for k in range(copies):
            x[k * count : (k + 1) * count, :] = rows_ref[k, 0, :, 0:width]
            dy[k * count : (k + 1) * count, :] = rows_ref[k, 0, :, width:]

    hidden, slope = gelu_parts(dotf(x[...], win_ref[0]))
    d_pre = (dotf(dy[...], wout_ref[0], ((1,), (1,))) * slope).astype(BF)
    gin_ref[0] = dotf(x[...], d_pre, ((0,), (0,)))
    gout_ref[0] = dotf(hidden.astype(BF), dy[...], ((0,), (0,)))


def expert_grads(rows, w_in, w_out):
    copies, local, count, double = rows.shape
    _, width, hidden = w_in.shape
    chunk = 256
    return pl.pallas_call(
        expert_grad_kernel,
        grid=(local, hidden // chunk),
        out_shape=(
            jax.ShapeDtypeStruct(w_in.shape, F32),
            jax.ShapeDtypeStruct(w_out.shape, F32),
        ),
        in_specs=[
            pl.BlockSpec((copies, 1, count, double), lambda e, f: (0, e, 0, 0)),
            pl.BlockSpec((1, width, chunk), lambda e, f: (e, 0, f)),
            pl.BlockSpec((1, chunk, width), lambda e, f: (e, f, 0)),
        ],
        out_specs=(
            pl.BlockSpec((1, width, chunk), lambda e, f: (e, 0, f)),
            pl.BlockSpec((1, chunk, width), lambda e, f: (e, f, 0)),
        ),
        scratch_shapes=[
            pltpu.VMEM((copies * count, width), BF),
            pltpu.VMEM((copies * count, width), BF),
        ],
        compiler_params=params(),
        cost_estimate=pl.CostEstimate(
            flops=8 * copies * local * count * width * hidden,
            bytes_accessed=12 * local * width * hidden,
            transcendentals=copies * local * count * hidden,
        ),
        name="expert_grads",
    )(rows, w_in, w_out)


def unmix_kernel(
    choices,
    res_ref, mix_ref, wts_ref, place_ref, ret_ref, gout_ref, att_ref, wo_ref, gain_ref, router_ref,
    pair_ref,
    out_ref, dres_ref, datt_ref, gproj_ref, small_ref,
    att, dproj, back,
):
    tokens, width = res_ref.shape
    experts = router_ref.shape[1]
    pairs = pair_ref.shape[1]
    rows_back = dotf(place_ref[...], ret_ref[...], ((0,), (0,))).astype(BF)
    y = rows_back[:, 0:width]
    dm = rows_back[:, width:]
    weight = wts_ref[...]
    low = weight.astype(BF)
    dw = dotf(y, gout_ref[...], ((1,), (1,))) + dotf(dm, mix_ref[...], ((1,), (1,)))
    d_chosen = weight * (dw - jnp.sum(weight * dw, axis=1, keepdims=True))
    pick = (
        lax.broadcasted_iota(jnp.int32, (experts, pairs), 0) == pair_ref[0:1, :]
    ).astype(BF)
    d_logits = dotf(pick, d_chosen.astype(BF)).astype(BF)
    small_ref[0:experts, :] = dotf(d_logits, mix_ref[...])
    small_ref[experts:, :] = jnp.zeros((small_ref.shape[0] - experts, width), F32)
    spare = back.shape[0] - pairs - experts
    back[0:pairs, :] = low
    back[pairs : pairs + experts, :] = d_logits
    if spare:
        back[pairs + experts :, :] = jnp.zeros((spare, tokens), BF)
    router_t = jnp.transpose(
        jnp.concatenate(
            [router_ref[...].astype(F32), jnp.zeros((width, 128 - experts), F32)], axis=1
        )
    ).astype(BF)[0 : back.shape[0] - pairs, :]
    for h in range(4):
        att[:, 128 * h : 128 * h + 128] = att_ref[h]
    rhs = jnp.concatenate([dm, router_t], axis=0)
    gain_grad = jnp.zeros((1, width), F32)
    for t in range(tokens // 256):
        rows = slice(t * 256, t * 256 + 256)
        res = res_ref[rows, :]
        combined = dotf(low[:, rows], y, ((0,), (0,)))
        out_ref[rows, :] = (res + combined).astype(BF)
        d_mix = dotf(back[:, rows], rhs, ((0,), (0,)))
        inv = lax.rsqrt(jnp.mean(res * res, axis=1, keepdims=True) + NORM_EPS)
        normed = res * inv
        scaled = d_mix * gain_ref[...]
        gain_grad = gain_grad + jnp.sum(d_mix * normed, axis=0, keepdims=True)
        inner = jnp.mean(scaled * normed, axis=1, keepdims=True)
        d_res = gout_ref[rows, :].astype(F32) + inv * (scaled - normed * inner)
        dres_ref[rows, :] = d_res
        d_low = d_res.astype(BF)
        dproj[rows, :] = d_low
        d_att = dotf(d_low, wo_ref[...], ((1,), (1,))).astype(BF)
        for h in range(4):
            datt_ref[h, rows, :] = d_att[:, 128 * h : 128 * h + 128]
    small_ref[experts : experts + 1, :] = gain_grad
    gproj_ref[...] = dotf(att[...], dproj[...], ((0,), (0,)))


def input_back_kernel(
    dqkv_ref, x_ref, gain_ref, w_ref, dres_ref, tg_ref, gq_ref, gg_ref, act, dqkv
):
    tokens, width = x_ref.shape
    for h in range(4):
        for i in range(3):
            first = i * width + 128 * h
            dqkv[:, first : first + 128] = dqkv_ref[h, :, 128 * i : 128 * i + 128]
    gain_grad = jnp.zeros((1, width), F32)
    for t in range(tokens // 256):
        rows = slice(t * 256, t * 256 + 256)
        x = x_ref[rows, :].astype(F32)
        inv = lax.rsqrt(jnp.mean(x * x, axis=1, keepdims=True) + NORM_EPS)
        normed = x * inv
        act[rows, :] = (normed * gain_ref[...]).astype(BF)
        d_act = dotf(dqkv[rows, :], w_ref[...], ((1,), (1,)))
        scaled = d_act * gain_ref[...]
        gain_grad = gain_grad + jnp.sum(d_act * normed, axis=0, keepdims=True)
        inner = jnp.mean(scaled * normed, axis=1, keepdims=True)
        tg_ref[rows, :] = dres_ref[rows, :] + inv * (scaled - normed * inner)
    gg_ref[...] = gain_grad
    for i in range(3):
        cols = slice(i * width, i * width + width)
        gq_ref[i] = dotf(act[...], dqkv[:, cols], ((0,), (0,)))


def reduce_kernel(
    planes, experts,
    gq_ref, gp_ref, small_ref, extra_ref,
    oq_ref, op_ref, os_ref,
    acc, wire, got0, got1, got2, quarter, gathered, half, slots,
    send0, send1, send2, recv0, recv1, recv2, back0, back1, back2, ssend, srecv,
):
    z = lax.axis_index("experts")
    c, d = coords()
    width = gp_ref.shape[0]
    eighth = got1.shape[1]
    piece = got2.shape[1]
    counts = (2, 4, planes)
    places = (d, c, z)
    axes = ("dp", "context", "experts")
    barrier = pltpu.get_barrier_semaphore()

    def mate(stage, k):
        return {axes[stage]: lax.rem(places[stage] + k, counts[stage])}

    total = 0
    for stage in range(3):
        for k in range(1, counts[stage]):
            pl.semaphore_signal(barrier, inc=1, device_id=mate(stage, k), device_id_type=MESH)
            total += 1
    pl.semaphore_wait(barrier, total)

    def copy(src, dst, send, recv, stage, k):
        return pltpu.make_async_remote_copy(
            src_ref=src, dst_ref=dst, send_sem=send, recv_sem=recv,
            device_id=mate(stage, k), device_id_type=MESH,
        )

    def small_start(stage, value):
        slots[stage, places[stage]] = value
        own = slots.at[stage, places[stage]]
        ops = [
            copy(own, own, ssend.at[stage, k - 1], srecv.at[stage, k - 1], stage, k)
            for k in range(1, counts[stage])
        ]
        for op in ops:
            op.start()
        return ops

    def small_sum(stage, ops):
        for op in ops:
            op.wait()
        value = slots[stage, 0]
        for k in range(1, counts[stage]):
            value = value + slots[stage, k]
        return value

    for i in range(4):
        source = gq_ref.at[i] if i < 3 else gp_ref
        rows = pl.ds((i % 2) * width, width)

        @pl.when(d == i // 2)
        def _():
            acc[rows, :] = source[...]

        @pl.when(d != i // 2)
        def _():
            wire[rows, :] = source[...].astype(BF)

    first = copy(wire, got0, send0, recv0, 0, 1)
    first.start()
    which = lax.broadcasted_iota(jnp.int32, small_ref.shape, 0)
    small = small_ref[...] + jnp.where(which == experts + 1, extra_ref[...], 0.0)
    small_ops = small_start(0, small)
    first.wait()
    acc[...] = acc[...] + got0[...].astype(F32)

    wire[...] = acc[...].astype(BF)
    ops = []
    for k in (2, 1, 3):
        other = lax.rem(c + k, 4)
        op = copy(
            wire.at[pl.ds(other * eighth, eighth)], got1.at[k - 1], send1.at[k - 1], recv1.at[k - 1], 1, k
        )
        op.start()
        ops.append(op)
    small_ops = small_start(1, small_sum(0, small_ops))
    for op in ops:
        op.wait()
    mine = acc[pl.ds(pl.multiple_of(c * eighth, eighth), eighth), :]
    for k in range(3):
        mine = mine + got1[k].astype(F32)
    acc[0:eighth, :] = mine
    quarter[...] = mine.astype(BF)
    ops = []
    for k in range(1, planes):
        other = lax.rem(z + k, planes)
        op = copy(
            quarter.at[pl.ds(other * piece, piece)], got2.at[k - 1], send2.at[k - 1], recv2.at[k - 1], 2, k
        )
        op.start()
        ops.append(op)
    small_ops = small_start(2, small_sum(1, small_ops))
    for op in ops:
        op.wait()
    mine = acc[pl.ds(pl.multiple_of(z * piece, piece), piece), :]
    for k in range(planes - 1):
        mine = mine + got2[k].astype(F32)

    own = pl.ds(pl.multiple_of(z * piece, piece), piece)
    plane_own = pl.ds(pl.multiple_of(c * eighth, eighth), eighth)
    gathered[own, :] = mine.astype(BF)
    ops = []
    for k in range(1, planes):
        op = copy(gathered.at[own], gathered.at[own], send2.at[k - 1], back2.at[k - 1], 2, k)
        op.start()
        ops.append(op)
    os_ref[...] = small_sum(2, small_ops)
    for op in ops:
        op.wait()

    half[d, plane_own, :] = gathered[...]
    ops = []
    for k in (2, 1, 3):
        op = copy(half.at[d, plane_own], half.at[d, plane_own], send1.at[k - 1], back1.at[k - 1], 1, k)
        op.start()
        ops.append(op)
    for op in ops:
        op.wait()

    last = copy(half.at[d], half.at[d], send0, back0, 0, 1)
    last.start()
    last.wait()
    for i in range(4):
        value = half[i // 2, (i % 2) * width : (i % 2 + 1) * width, :].astype(F32)
        if i < 3:
            oq_ref[:, i * width : (i + 1) * width] = value
        else:
            op_ref[...] = value


def reduce_all(gq, gp, small, extra, planes, experts):
    width = gp.shape[0]
    eighth = width // 2
    piece = eighth // planes
    most = max(4, planes)
    dma = pltpu.SemaphoreType.DMA
    return pl.pallas_call(
        functools.partial(reduce_kernel, planes, experts),
        out_shape=(
            jax.ShapeDtypeStruct((width, 3 * width), F32),
            jax.ShapeDtypeStruct((width, width), F32),
            jax.ShapeDtypeStruct(small.shape, F32),
        ),
        in_specs=[VMEM] * 4,
        out_specs=(VMEM,) * 3,
        scratch_shapes=[
            pltpu.VMEM((2 * width, width), F32),
            pltpu.VMEM((2 * width, width), BF),
            pltpu.VMEM((2 * width, width), BF),
            pltpu.VMEM((3, eighth, width), BF),
            pltpu.VMEM((planes - 1, piece, width), BF),
            pltpu.VMEM((eighth, width), BF),
            pltpu.VMEM((eighth, width), BF),
            pltpu.VMEM((2, 2 * width, width), BF),
            pltpu.VMEM((3, most) + small.shape, F32),
            dma, dma((3,)), dma((planes - 1,)),
            dma, dma((3,)), dma((planes - 1,)),
            dma, dma((3,)), dma((planes - 1,)),
            dma((3, most - 1)), dma((3, most - 1)),
        ],
        compiler_params=params(collective_id=5, has_side_effects=True),
        name="reduce_all",
    )(gq, gp, small, extra)


def pick_rows(sources, local, capacity, stride):
    pick = np.zeros((local, sources * capacity, sources * stride), np.float32)
    for e in range(local):
        for r in range(sources * capacity):
            pick[e, r, (r // capacity) * stride + e * capacity + r % capacity] = 1.0
    return pick


def per_device(
    planes,
    tokens,
    attn_gain,
    mix_gain,
    query_key_value_weight,
    output_weight,
    router_weight,
    w_in,
    w_exp_out,
    out_grad,
    group_slot,
    group_routes,
    route_order,
):
    x = tokens[0]
    gout = out_grad[0]
    count, width = x.shape
    groups, choices = group_routes.shape
    pairs = groups * choices
    experts = router_weight.shape[1]
    local = w_in.shape[0]
    sources = experts // local
    capacity = 5 * groups * choices // (4 * experts)
    stride = -(-local * capacity // 16) * 16
    slots = sources * stride
    small_rows = -(-(experts + 2) // 8) * 8
    gain_one = attn_gain.reshape(1, width)
    gain_two = mix_gain.reshape(1, width)
    pair_table = jnp.stack([group_routes.reshape(-1), route_order.reshape(-1)])

    sequence = gather_tokens(x, 4).reshape(4 * count, width)
    qkv, o, lse = attention(sequence, gain_one, query_key_value_weight)
    att = to_home(o.reshape(4, count, 128), 1)

    res, mix, weights, place, send = pl.pallas_call(
        functools.partial(mix_kernel, stride, capacity, local, choices),
        out_shape=(
            jax.ShapeDtypeStruct((count, width), F32),
            jax.ShapeDtypeStruct((count, width), BF),
            jax.ShapeDtypeStruct((pairs, count), F32),
            jax.ShapeDtypeStruct((slots, pairs), BF),
            jax.ShapeDtypeStruct((slots, 2 * width), BF),
        ),
        in_specs=[VMEM] * 8,
        out_specs=(VMEM,) * 5,
        scratch_shapes=[pltpu.VMEM((count, width), BF)],
        compiler_params=params(),
        name="mix",
    )(x, att, output_weight, gain_two, router_weight, group_slot, pair_table, gout)

    recv = lax.all_to_all(
        send.reshape(sources, stride, 2 * width), "experts", split_axis=0, concat_axis=0, tiled=True
    ).reshape(slots, 2 * width)
    pick = jnp.asarray(pick_rows(sources, local, capacity, stride), BF)
    rows, ret = expert_rows(recv, pick, w_in, w_exp_out)
    ret = lax.all_to_all(
        ret.reshape(sources, stride, 2 * width), "experts", split_axis=0, concat_axis=0, tiled=True
    ).reshape(slots, 2 * width)
    all_rows = lax.all_gather(rows, ("context", "dp"), axis=0)

    layer_out, d_res, d_att, g_proj, small = pl.pallas_call(
        functools.partial(unmix_kernel, choices),
        out_shape=(
            jax.ShapeDtypeStruct((count, width), BF),
            jax.ShapeDtypeStruct((count, width), F32),
            jax.ShapeDtypeStruct((4, count, 128), BF),
            jax.ShapeDtypeStruct((width, width), F32),
            jax.ShapeDtypeStruct((small_rows, width), F32),
        ),
        in_specs=[VMEM] * 11,
        out_specs=(VMEM,) * 5,
        scratch_shapes=[
            pltpu.VMEM((count, width), BF),
            pltpu.VMEM((count, width), BF),
            pltpu.VMEM((pairs + -(-experts // 16) * 16, count), BF),
        ],
        compiler_params=params(),
        name="unmix",
    )(
        res, mix, weights, place, ret, gout, att, output_weight, gain_two, router_weight, pair_table
    )

    d_o = to_heads(d_att, 2).reshape(4 * count, 128)
    d_heads = attention_back(qkv, d_o, o, lse)
    d_qkv = to_home(d_heads.reshape(4, count, 384), 3)
    token_grad, g_qkv, g_one = pl.pallas_call(
        input_back_kernel,
        out_shape=(
            jax.ShapeDtypeStruct((count, width), F32),
            jax.ShapeDtypeStruct((3, width, width), F32),
            jax.ShapeDtypeStruct((1, width), F32),
        ),
        in_specs=[VMEM] * 5,
        out_specs=(VMEM,) * 3,
        scratch_shapes=[pltpu.VMEM((count, width), BF), pltpu.VMEM((count, 3 * width), BF)],
        compiler_params=params(),
        name="input_back",
    )(d_qkv, x, gain_one, query_key_value_weight, d_res)
    g_in, g_out = expert_grads(all_rows, w_in, w_exp_out)
    qkv_grad, proj_grad, small = reduce_all(g_qkv, g_proj, small, g_one, planes, experts)
    return (
        layer_out[None],
        token_grad[None],
        small[experts + 1],
        small[experts],
        qkv_grad,
        proj_grad,
        jnp.transpose(small[:experts]),
        g_in,
        g_out,
    )


def solution(mesh):
    token_spec = P(("experts", "dp"), "context", None)
    pair_spec = P(("experts", "context", "dp"), None)
    expert_spec = P("experts", None, None)
    return jax.shard_map(
        functools.partial(per_device, mesh.shape["experts"]),
        mesh=mesh,
        in_specs=(
            token_spec, P(), P(), P(), P(), P(), expert_spec, expert_spec, token_spec,
            P(("experts", "dp"), "context"), pair_spec, pair_spec,
        ),
        out_specs=(
            token_spec, token_spec, P(), P(), P(), P(), P(), expert_spec, expert_spec,
        ),
        check_vma=False,
    )
```

time: 1080 us -> 374 us (0.35)
  waiting for transfers between devices: 490 us -> 0.02 us
  Pallas kernels: 0 us -> 322 us
  local copies, waits for them, and re-layouts: 192 us -> 8.85 us
  matrix products: 139 us -> 0 us
  starting transfers between devices: 136 us -> 0.04 us
  other arithmetic: 54.6 us -> 0.57 us
  blocking collectives: 40 us -> 26.9 us
    ppermute x3 -> x0, waiting for transfers between devices: 333 us -> none  [passed_along(): return lax.ppermute(block, axis, route)]
    pallas_call x0 -> x12, Pallas kernels: none -> 322 us  [the longest x1 61.6 us: attention_back(): pl.pallas_call(attention_back_kernel, out_shape=jax.ShapeDtypeStruct((len...]
    dot_general x36 -> x0, matrix products: 139 us -> none  [the longest x2 21.3 us: back_visit_block(): jnp.einsum('hqk,qhd->khd', probs_full.astype(jnp.bfloat16), grad_heads, p...]
    ppermute x3 -> x0, starting transfers between devices: 120 us -> none  [passed_along(): return lax.ppermute(block, axis, route)]
    psum x2 -> x0, waiting for transfers between devices: 77.8 us -> none  [the longest x1 77.8 us: per_device(): lax.psum((attn_gain_grad, mix_gain_grad, qkv_grad, out_proj_grad, route_g...]
    gather x15 -> x0, local copies, waits for them, and re-layouts: 75.2 us -> none  [the longest x5 35.7 us: per_device(): chosen = jnp.take_along_axis(grouped_logit, route_index, axis=2)]
    all_gather x1, waiting for transfers between devices: 69.2 us -> 0.01 us  [per_device(): all_rows = lax.all_gather(rows, ('context', 'dp'), axis=0)]
    psum x1 -> x0, blocking collectives: 40 us -> none  [per_device(): lax.psum((attn_gain_grad, mix_gain_grad, qkv_grad, out_proj_grad, route_g...]
  transfers between devices with their start and end apart: 10 -> 1, of which waited for: 9 -> 0; matrix products, arithmetic and copies ran while one was open for 24% -> 1% of each run, Pallas kernels for 0% -> 51%
where the time goes in v1:
time: 374 us; the launch traced here: 372 us
  Pallas kernels  322 us (86%)
  blocking collectives  26.9 us (7%)
  between operations  14.1 us (4%)
  local copies, waits for them, and re-layouts  8.85 us (2%)
    pallas_call x1, Pallas kernels, attention_back(): pl.pallas_call(attention_back_kernel, out_shape=jax.ShapeDtypeStruct((len...  61.6 us
    pallas_call x2, Pallas kernels, to_home(): pl.pallas_call(home_kernel, out_shape=jax.ShapeDtypeStruct(x.shape, x.dty...  54.8 us
    pallas_call x1, Pallas kernels, reduce_all(): pl.pallas_call(functools.partial(reduce_kernel, planes, experts), out_sha...  52.3 us
    pallas_call x1, Pallas kernels, attention(): pl.pallas_call(attention_kernel, out_shape=(jax.ShapeDtypeStruct((length,...  39.1 us
    pallas_call x1, Pallas kernels, gather_tokens(): pl.pallas_call(gather_kernel, out_shape=jax.ShapeDtypeStruct((context,) +...  36.9 us
    pallas_call x1, Pallas kernels, expert_grads(): pl.pallas_call(expert_grad_kernel, grid=(local, hidden // chunk), out_sha...  24.1 us
    pallas_call x1, Pallas kernels, to_heads(): pl.pallas_call(heads_kernel, out_shape=jax.ShapeDtypeStruct(x.shape, x.dt...  18.7 us
    all_to_all x1, blocking collectives, per_device(): lax.all_to_all(send.reshape(sources, stride, 2 * width), 'experts', split...  13.9 us
  transfers between devices with their start and end apart: 1, of which 0 were waited for; matrix products, arithmetic and copies ran while one was open for 1% of the time, Pallas kernels for 51%

profile of v1, /device:TPU:0, one launch (start us, length us, event | category | flops | bytes accessed | tf_op | source)
XLA Modules:
  0.0 372.3 jit_solution(6187558249478511590)
XLA Ops:
  7.2 0.8 copy.30
  8.0 0.1 stack_reshape.6
  8.1 0.8 copy.31
  9.0 1.5 copy.32.router_ref
  10.4 36.9 %shard_map.196 = bf16[4,1024,512]{2,1,0:T(8,128)(2,1)} custom-call(bf16[1024,512]{1,0:T(8,128)(2,1)} %bitcast.21), custom_call_target="tpu_custom_call" | custom-call | tf_op jit(solution)/shard_map/pallas_call | solution.py:126
  47.4 39.1 %attention.1 = (bf16[4096,384]{1,0:T(8,128)(2,1)}, bf16[4096,128]{1,0:T(8,128)(2,1)}, f32[2,4096]{1,0:T(2,128)}) custom-call(bf16[4096,512]{1,0:T(8,128)(2,1)} %bitcast.19, f32[1,512]{1,0:T(1,128)} %bitcast.34, bf16[512,1536]{1,0:T(8,128)(2,1)} %w_ref.3), custom_call_target="tpu_custom_call" | custom-call | tf_op jit(solution)/shard_map/attention/pallas_call | solution.py:319
  86.5 15.6 %shard_map.197.att_ref = bf16[4,1024,128]{2,1,0:T(8,128)(2,1)} custom-call(bf16[4,1024,128]{2,1,0:T(8,128)(2,1)} %bitcast.26), custom_call_target="tpu_custom_call" | custom-call | tf_op jit(solution)/shard_map/pallas_call | solution.py:182
  102.0 0.6 pad_add_fusion.pair_ref
  102.6 6.2 %mix.1 = (f32[1024,512]{1,0:T(8,128)}, bf16[1024,512]{1,0:T(8,128)(2,1)}, f32[128,1024]{1,0:T(8,128)}, bf16[192,128]{1,0:T(8,128)(2,1)}, bf16[192,1024]{1,0:T(8,128)(2,1)}) custom-call(bf16[1024,512]{1,0:T(8,128)(2,1)} %bitcast.22, bf16[4,1024,128]{2,1,0:T(8,128)(2,1)} %shard_map.197.att_ref, bf16[512,512]{1,0:T(8,128)(2,1)} %wo_ref.3, f32[1,512]{1,0:T(1,128)} %bitcast.32, ...), custom_call_target="tpu_custom_call" | custom-call | tf_op jit(solution)/shard_map/mix/pallas_call | solution.py:903
  108.8 13.9 %all_to_all.10 = bf16[4,48,1024]{2,1,0:T(8,128)(2,1)} all-to-all(bf16[4,48,1024]{2,1,0:T(8,128)(2,1)} %bitcast.31), channel_id=1, replica_groups=mesh['experts'=4,'context'=4,'dp'=2] {'experts'}, dimensions={0} | all-to-all | bytes 786432 | tf_op jit(solution)/shard_map/all_to_all | solution.py:919
  122.6 10.8 %expert_rows.1 = (bf16[2,80,1024]{2,1,0:T(8,128)(2,1)}, bf16[192,1024]{1,0:T(8,128)(2,1)}) custom-call(bf16[192,1024]{1,0:T(8,128)(2,1)} %bitcast.28, bf16[2,80,192]{2,1,0:T(8,128)(2,1)} %constant.2.clone.pick_ref, bf16[2,512,2048]{2,1,0:T(8,128)(2,1)} %win_ref.3, bf16[2,2048,512]{2,1,0:T(8,128)(2,1)} %wout_ref.3), custom_call_target="tpu_custom_call" | custom-call | tf_op jit(solution)/shard_map/expert_rows/pallas_call | solution.py:531
  133.5 13.1 %all_to_all.11 = bf16[4,48,1024]{2,1,0:T(8,128)(2,1)} all-to-all(bf16[4,48,1024]{2,1,0:T(8,128)(2,1)} %bitcast.30), channel_id=1, replica_groups=mesh['experts'=4,'context'=4,'dp'=2] {'experts'}, dimensions={0} | all-to-all | bytes 786432 | tf_op jit(solution)/shard_map/all_to_all | solution.py:924
  146.6 8.4 %unmix.1 = (bf16[1024,512]{1,0:T(8,128)(2,1)}, f32[1024,512]{1,0:T(8,128)}, bf16[4,1024,128]{2,1,0:T(8,128)(2,1)}, f32[512,512]{1,0:T(8,128)}, f32[16,512]{1,0:T(8,128)}) custom-call(f32[1024,512]{1,0:T(8,128)} %get-tuple-element.33.res_ref, bf16[1024,512]{1,0:T(8,128)(2,1)} %get-tuple-element.34.mix_ref, f32[128,1024]{1,0:T(8,128)} %get-tuple-element.35.wts_ref, ...), custom_call_target="tpu_custom_call" | custom-call | tf_op jit(solution)/shard_map/unmix/pallas_call | solution.py:929
  155.0 18.7 %shard_map.198 = bf16[4,1024,128]{2,1,0:T(8,128)(2,1)} custom-call(bf16[4,1024,128]{2,1,0:T(8,128)(2,1)} %get-tuple-element.41.x_ref), custom_call_target="tpu_custom_call" | custom-call | tf_op jit(solution)/shard_map/pallas_call | solution.py:235
  173.7 61.6 %attention_back.1 = bf16[4096,384]{1,0:T(8,128)(2,1)} custom-call(bf16[4096,384]{1,0:T(8,128)(2,1)} %get-tuple-element.40.qkv_ref, bf16[4096,128]{1,0:T(8,128)(2,1)} %bitcast.27, bf16[4096,128]{1,0:T(8,128)(2,1)} %get-tuple-element.32.o_ref, f32[2,4096]{1,0:T(2,128)} %get-tuple-element.42.lse_ref), custom_call_target="tpu_custom_call" | custom-call | tf_op jit(solution)/shard_map/attention_back/pallas_call | solution.py:410
  235.2 39.3 %shard_map.199.dqkv_ref = bf16[4,1024,384]{2,1,0:T(8,128)(2,1)} custom-call(bf16[4,1024,384]{2,1,0:T(8,128)(2,1)} %bitcast.20), custom_call_target="tpu_custom_call" | custom-call | tf_op jit(solution)/shard_map/pallas_call | solution.py:182
  274.5 8.9 %input_back.1 = (f32[1024,512]{1,0:T(8,128)}, f32[3,512,512]{2,1,0:T(8,128)}, f32[1,512]{1,0:T(1,128)}) custom-call(bf16[4,1024,384]{2,1,0:T(8,128)(2,1)} %shard_map.199.dqkv_ref, bf16[1024,512]{1,0:T(8,128)(2,1)} %bitcast.23, f32[1,512]{1,0:T(1,128)} %bitcast.35, bf16[512,1536]{1,0:T(8,128)(2,1)} %w_ref.3, f32[1024,512]{1,0:T(8,128)} %get-tuple-element.43.dres_ref), custom_call_target="tpu_custom_call" | custom-call | tf_op jit(solution)/shard_map/input_back/pallas_call | solution.py:954
  283.4 52.3 %reduce_all.1 = (f32[512,1536]{1,0:T(8,128)}, f32[512,512]{1,0:T(8,128)}, f32[16,512]{1,0:T(8,128)}) custom-call(f32[3,512,512]{2,1,0:T(8,128)} %get-tuple-element.45.gq_ref, f32[512,512]{1,0:T(8,128)} %get-tuple-element.46.gp_ref, f32[16,512]{1,0:T(8,128)} %get-tuple-element.47.small_ref, f32[1,512]{1,0:T(1,128)} %get-tuple-element.48.extra_ref), custom_call_target="tpu_custom_call" | custom-call | tf_op jit(solution)/shard_map/reduce_all/pallas_call | solution.py:831
  335.8 1.4 fusion
  337.1 1.3 slice_bitcast_fusion
  338.5 24.1 %expert_grads.1 = (f32[2,512,2048]{2,1,0:T(8,128)}, f32[2,2048,512]{2,1,0:T(8,128)}) custom-call(bf16[8,2,80,1024]{3,2,1,0:T(8,128)(2,1)} %bitcast.38, bf16[2,512,2048]{2,1,0:T(8,128)(2,1)} %win_ref.3, bf16[2,2048,512]{2,1,0:T(8,128)(2,1)} %wout_ref.3), custom_call_target="tpu_custom_call" | custom-call | flops 10737418240 | bytes 25165824 | tf_op jit(solution)/shard_map/expert_grads/pallas_call | solution.py:574
  362.5 1.7 copy.36
  364.2 0.3 copy-done.1
  364.5 1.0 copy.37
  (7 shorter events, 0.2 us)
Async XLA Ops:
  7.2 331.3 %all-gather.3.cloned.1.call-start = ((), (), s32[]{:S(2)}) async-start(), calls=%async_computation.2 | async-start | bytes 2949120 | tf_op jit(solution)/shard_map/all_gather | solution.py:927
  338.5 24.1 %copy-start = (f32[512,1536]{1,0:T(8,128)S(1)}, f32[512,1536]{1,0:T(8,128)}, u32[]{:S(2)}) copy-start(f32[512,1536]{1,0:T(8,128)} %get-tuple-element.70) | copy-start | bytes 9437188
  362.5 2.0 copy-start.1
Sparse Core Ops, SparseCore 0:
  133.6 30.1 all-gather.2

commit v2 on v1

--- a/solution.py
+++ b/solution.py
@@ -193,60 +193,7 @@
     )(x)
 
 
-def heads_kernel(x_ref, o_ref, local, send, recv):
-    c, d = coords()
-    seq = sequence_of(c)
-    plane_barrier(c, d)
-    for h in range(4):
-        chip = chip_of(d, h // 2)
-        e = h % 2
-        own = jnp.logical_and(chip == c, e == d)
-
-        @pl.when(own)
-        def _():
-            pltpu.make_async_copy(x_ref.at[h], o_ref.at[c], local).start()
-
-        @pl.when(jnp.logical_not(own))
-        def _():
-            remote(x_ref.at[h], o_ref.at[c], send.at[h], recv.at[c], chip, e).start()
-
-    for h in range(4):
-        chip = chip_of(d, h // 2)
-        e = h % 2
-        own = jnp.logical_and(chip == c, e == d)
-
-        @pl.when(own)
-        def _():
-            pltpu.make_async_copy(x_ref.at[h], o_ref.at[c], local).wait()
-
-        @pl.when(jnp.logical_not(own))
-        def _():
-            remote(x_ref.at[h], o_ref.at[c], send.at[h], recv.at[c], chip, e).wait_send()
-
-    for b in range(4):
-        own = jnp.logical_and(b == c, d == seq)
-
-        @pl.when(jnp.logical_not(own))
-        def _():
-            remote(x_ref.at[b], o_ref.at[b], send.at[b], recv.at[b], c, d).wait_recv()
-
-
-def to_heads(x, cid):
-    return pl.pallas_call(
-        heads_kernel,
-        out_shape=jax.ShapeDtypeStruct(x.shape, x.dtype),
-        in_specs=[ANY],
-        out_specs=ANY,
-        scratch_shapes=[
-            pltpu.SemaphoreType.DMA,
-            pltpu.SemaphoreType.DMA((4,)),
-            pltpu.SemaphoreType.DMA((4,)),
-        ],
-        compiler_params=params(collective_id=cid, has_side_effects=True),
-    )(x)
-
-
-def attention_kernel(x_ref, gain_ref, w_ref, qkv_ref, o_ref, lse_ref, ws, vx, acc):
+def attention_kernel(x_ref, gain_ref, w_ref, qkv_ref, o_ref, lse_ref, act_ref, ws, vx, acc):
     length = x_ref.shape[0]
     tq, tk = 1024, 512
     c, e = coords()
@@ -265,6 +212,7 @@
         x = x_ref[rows, :].astype(F32)
         inv = lax.rsqrt(jnp.mean(x * x, axis=1, keepdims=True) + NORM_EPS)
         act = (x * inv * gain_ref[...]).astype(BF)
+        act_ref[rows, :] = act
         qkv = dotf(act, ws[...]).astype(BF)
         qkv_ref[rows, 0:128] = qkv[:, 0:128] * jnp.asarray(0.125, BF)
         qkv_ref[rows, 128:384] = qkv[:, 128:384]
@@ -322,9 +270,10 @@
             jax.ShapeDtypeStruct((length, 384), BF),
             jax.ShapeDtypeStruct((length, 128), BF),
             jax.ShapeDtypeStruct((2, length), F32),
+            jax.ShapeDtypeStruct(x.shape, BF),
         ),
         in_specs=[VMEM] * 3,
-        out_specs=(VMEM,) * 3,
+        out_specs=(VMEM,) * 4,
         scratch_shapes=[
             pltpu.VMEM((w.shape[0], 384), BF),
             pltpu.VMEM((2, 80, length), BF),
@@ -335,9 +284,73 @@
     )(x, gain, w)
 
 
-def attention_back_kernel(qkv_ref, do_ref, o_ref, lse_ref, d_ref, qh, dh, kh, dq, delta):
+def back_kernel(
+    planes,
+    datt_ref, qkv_ref, o_ref, lse_ref, act_ref, x_ref, gain_ref, w_ref, dres_ref, gp_ref, small_ref,
+    tg_ref, oq_ref, op_ref, os_ref, gg_ref,
+    do, qh, dh, kh, dq, dkv, delta, dsend, dhome, gq, dall,
+    wire0, got0, wire1, got1, all2, sum1, back1, slots,
+    wire3, got3, sum3, got4, back4, final,
+    local, dsems, drecv, hsems, hrecv,
+    send0, send1, send2, recv0, recv1, recv2, ret0, ret1, ssend, srecv,
+    bsend, brecv, csend, crecv, cback, fsend, frecv, gsend, grecv,
+):
+    z = lax.axis_index("experts")
+    c, d = coords()
+    seq = sequence_of(c)
+    column = lax.rem(c, 2)
+    pair = 2 * (c // 2) + d
+    side = 2 * (c // 2) + 1 - column
+    over = 2 * (1 - c // 2) + column
+    far = 3 - c
+    native = d == seq
     length = qkv_ref.shape[0]
+    block = length // 4
+    width = gain_ref.shape[1]
     tq = tk = TILE
+    tiles = length // TILE
+    per = block // TILE
+    counts = (2, 4, planes)
+    places = (d, c, z)
+    axes = ("dp", "context", "experts")
+
+    def mate(stage, k):
+        return {axes[stage]: lax.rem(places[stage] + k, counts[stage])}
+
+    barrier = pltpu.get_barrier_semaphore()
+    for k in range(1, 8):
+        other = lax.rem(2 * c + d + k, 8)
+        pl.semaphore_signal(
+            barrier, inc=1, device_id={"context": other // 2, "dp": lax.rem(other, 2)},
+            device_id_type=MESH,
+        )
+    for k in range(1, planes):
+        pl.semaphore_signal(barrier, inc=1, device_id=mate(2, k), device_id_type=MESH)
+    pl.semaphore_wait(barrier, 6 + planes)
+
+    def copy(src, dst, send, recv, stage, k):
+        return pltpu.make_async_remote_copy(
+            src_ref=src, dst_ref=dst, send_sem=send, recv_sem=recv,
+            device_id=mate(stage, k), device_id_type=MESH,
+        )
+
+    def scatter(h, go):
+        chip = chip_of(d, h // 2)
+        e = h % 2
+        own = jnp.logical_and(chip == c, e == d)
+
+        @pl.when(jnp.logical_and(own, go))
+        def _():
+            pltpu.make_async_copy(datt_ref.at[h], do.at[c], local.at[0]).start()
+
+        @pl.when(jnp.logical_not(own))
+        def _():
+            op = remote(datt_ref.at[h], do.at[c], dsems.at[h], drecv.at[c], chip, e)
+            op.start() if go else op.wait_send()
+
+    for h in range(4):
+        scatter(h, True)
+
     low = lax.broadcasted_iota(jnp.int32, (1, 128), 1) < 64
     low_rows = lax.broadcasted_iota(jnp.int32, (128, 1), 0) < 64
     head_sum = (
@@ -345,29 +358,141 @@
         == lax.broadcasted_iota(jnp.int32, (8, 128), 0)
     ).astype(F32)
 
-    @pl.loop(0, length // TILE)
+    @pl.loop(0, tiles)
     def _(t):
         rows = pl.ds(pl.multiple_of(t * TILE, TILE), TILE)
         q = qkv_ref[rows, 0:128]
-        g = do_ref[rows, :]
-        z = jnp.zeros_like(q)
-        qh[0, rows, :] = jnp.where(low, q, z)
-        qh[1, rows, :] = jnp.where(low, z, q)
-        dh[0, rows, :] = jnp.where(low, g, z)
-        dh[1, rows, :] = jnp.where(low, z, g)
+        zero = jnp.zeros_like(q)
+        qh[0, rows, :] = jnp.where(low, q, zero)
+        qh[1, rows, :] = jnp.where(low, zero, q)
         kt = jnp.transpose(qkv_ref[rows, 128:256].astype(F32)).astype(BF)
         zt = jnp.zeros_like(kt)
         kh[0, :, rows] = jnp.where(low_rows, kt, zt)
         kh[1, :, rows] = jnp.where(low_rows, zt, kt)
-        product = g.astype(F32) * o_ref[rows, :].astype(F32)
-        delta[:, rows] = dotf(
-            head_sum, product, ((1,), (1,)), precision=lax.Precision.HIGHEST
-        )
         dq[:, rows] = jnp.zeros((128, TILE), F32)
-
-    def step(i, j, k, v, masked):
+        dkv[rows, :] = jnp.zeros((TILE, 256), F32)
+
+    gq[...] = jnp.zeros_like(gq)
+
+    width_half = width // 2
+    eighth = width_half // 4
+
+    def small_start(stage, value):
+        slots[stage, places[stage]] = value
+        own = slots.at[stage, places[stage]]
+        for k in range(1, counts[stage]):
+            copy(own, own, ssend.at[stage, k - 1], srecv.at[stage, k - 1], stage, k).start()
+
+    def small_sum(stage):
+        own = slots.at[stage, places[stage]]
+        for k in range(1, counts[stage]):
+            copy(own, own, ssend.at[stage, k - 1], srecv.at[stage, k - 1], stage, k).wait()
+        value = slots[stage, 0]
+        for k in range(1, counts[stage]):
+            value = value + slots[stage, k]
+        return value
+
+    def stage0():
+        return copy(wire0, got0, send0, recv0, 0, 1)
+
+    def stage1(k):
+        rows = pl.ds(lax.rem(c + k, 4) * eighth, eighth)
+        return copy(wire1.at[rows], got1.at[k - 1], send1.at[k - 1], recv1.at[k - 1], 1, k)
+
+    def stage2(k):
+        return copy(all2.at[z], all2.at[z], send2.at[k - 1], recv2.at[k - 1], 2, k)
+
+    own1 = pl.ds(pl.multiple_of(c * eighth, eighth), eighth)
+
+    def stage4(k):
+        return copy(back1.at[d, own1], back1.at[d, own1], send1.at[k - 1], ret1.at[k - 1], 1, k)
+
+    def stage5():
+        return copy(back1.at[d], back1.at[d], send0, ret0, 0, 1)
+
+    def early(t):
+        @pl.when(t == 0)
+        def _():
+            wire0[...] = gp_ref[pl.ds(pl.multiple_of((1 - d) * width_half, width_half), width_half), :].astype(BF)
+            stage0().start()
+            small_start(0, small_ref[...])
+
+        @pl.when(t == 1)
+        def _():
+            stage0().wait()
+            mine = gp_ref[pl.ds(pl.multiple_of(d * width_half, width_half), width_half), :] + got0[...].astype(F32)
+            sum1[...] = mine
+            wire1[...] = mine.astype(BF)
+            for k in (2, 1, 3):
+                stage1(k).start()
+            small_start(1, small_sum(0))
+
+        @pl.when(t == 2)
+        def _():
+            for k in range(1, 4):
+                stage1(k).wait()
+            mine = sum1[own1, :]
+            for k in range(3):
+                mine = mine + got1[k].astype(F32)
+            all2[z] = mine.astype(BF)
+            for k in range(1, planes):
+                stage2(k).start()
+            small_start(2, small_sum(1))
+
+        @pl.when(t == 3)
+        def _():
+            for k in range(1, planes):
+                stage2(k).wait()
+            mine = all2[0].astype(F32)
+            for k in range(1, planes):
+                mine = mine + all2[k].astype(F32)
+            back1[d, own1, :] = mine.astype(BF)
+            for k in (2, 1, 3):
+                stage4(k).start()
+            os_ref[...] = small_sum(2)
+
+        @pl.when(t == 4)
+        def _():
+            for k in range(1, 4):
+                stage4(k).wait()
+            stage5().start()
+
+        @pl.when(t == 5)
+        def _():
+            stage5().wait()
+            for i in range(2):
+                op_ref[i * width_half : (i + 1) * width_half, :] = back1[i].astype(F32)
+
+    for source in (c, side, over, far):
+        if source is c:
+            @pl.when(native)
+            def _():
+                pltpu.make_async_copy(datt_ref.at[0], do.at[c], local.at[0]).wait()
+
+            @pl.when(jnp.logical_not(native))
+            def _():
+                remote(do.at[c], do.at[c], dsems.at[0], drecv.at[c], c, d).wait_recv()
+        else:
+            remote(do.at[source], do.at[source], dsems.at[0], drecv.at[source], c, d).wait_recv()
+
+        @pl.loop(0, per)
+        def _(t):
+            part = pl.ds(pl.multiple_of(t * TILE, TILE), TILE)
+            rows = pl.ds(pl.multiple_of(source * block + t * TILE, TILE), TILE)
+            g = do[source, part, :]
+            zero = jnp.zeros_like(g)
+            dh[0, rows, :] = jnp.where(low, g, zero)
+            dh[1, rows, :] = jnp.where(low, zero, g)
+            product = g.astype(F32) * o_ref[rows, :].astype(F32)
+            delta[:, rows] = dotf(
+                head_sum, product, ((1,), (1,)), precision=lax.Precision.HIGHEST
+            )
+
+    def step(i, j, masked):
         qrows = pl.ds(pl.multiple_of(i * tq, tq), tq)
         krows = pl.ds(pl.multiple_of(j * tk, tk), tk)
+        k = qkv_ref[krows, 128:256]
+        v = qkv_ref[krows, 256:384]
         dk = dv = dqt = 0.0
         for h in range(2):
             s = dotf(k, qh[h, qrows, :], ((1,), (1,)))
@@ -382,46 +507,204 @@
             dk = dk + dotf(ds, qh[h, qrows, :])
             dqt = dqt + dotf(kh[h, :, krows], ds)
         dq[:, qrows] = dq[:, qrows] + dqt
-        return dk, dv
-
-    @pl.loop(0, length // tk)
-    def _(j):
-        krows = pl.ds(pl.multiple_of(j * tk, tk), tk)
-        k = qkv_ref[krows, 128:256]
-        v = qkv_ref[krows, 256:384]
-        first = step(j, j, k, v, True)
-
-        def body(i, carry):
-            dk, dv = step(i, j, k, v, False)
-            return carry[0] + dk, carry[1] + dv
-
-        dk, dv = lax.fori_loop(j + 1, length // tq, body, first)
-        d_ref[krows, 128:256] = dk.astype(BF)
-        d_ref[krows, 256:384] = dv.astype(BF)
-
-    @pl.loop(0, length // TILE)
+        dkv[krows, 0:128] = dkv[krows, 0:128] + dk
+        dkv[krows, 128:256] = dkv[krows, 128:256] + dv
+
+    def send_home(b, go):
+        own = jnp.logical_and(b == c, native)
+
+        @pl.when(own)
+        def _():
+            op = pltpu.make_async_copy(dsend.at[b], dhome.at[pair], local.at[1])
+            op.start() if go else op.wait()
+
+        @pl.when(jnp.logical_not(own))
+        def _():
+            op = remote(dsend.at[b], dhome.at[pair], hsems.at[b], hrecv.at[pair], b, seq)
+            op.start() if go else op.wait_send()
+
+    @pl.loop(0, tiles)
     def _(t):
-        rows = pl.ds(pl.multiple_of(t * TILE, TILE), TILE)
-        d_ref[rows, 0:128] = (jnp.transpose(dq[:, rows]) * 0.125).astype(BF)
-
-
-def attention_back(qkv, do, o, lse):
+        early(t)
+        diagonal = jnp.where(d == 0, t, tiles - 1 - t)
+        step(diagonal, diagonal, True)
+
+        @pl.loop(1, tiles - t)
+        def _(u):
+            step(
+                jnp.where(d == 0, t + u, tiles - 1 - t),
+                jnp.where(d == 0, t, tiles - 1 - t - u),
+                False,
+            )
+
+        @pl.when(lax.rem(t, per) == per - 1)
+        def _():
+            b = diagonal // per
+            for half in range(per):
+                rows = pl.ds(pl.multiple_of(b * block + half * TILE, TILE), TILE)
+                part = slice(half * TILE, half * TILE + TILE)
+                dsend[b, part, 0:128] = (jnp.transpose(dq[:, rows]) * 0.125).astype(BF)
+                dsend[b, part, 128:384] = dkv[rows, :].astype(BF)
+            for k in range(4):
+                @pl.when(b == k)
+                def _():
+                    send_home(k, True)
+            rows = pl.ds(pl.multiple_of(b * block, block), block)
+            gq[...] = gq[...] + dotf(act_ref[rows, :], dsend[b], ((0,), (0,)))
+
+    rest = gq.shape[0] // 2
+    bit = rest // planes
+
+    def next0():
+        return remote(wire3, got3, bsend, brecv, side, d)
+
+    def next1(k):
+        rows = pl.ds(lax.rem(z + k, planes) * bit, bit)
+        return copy(wire3.at[rows], got4.at[k - 1], csend.at[k - 1], crecv.at[k - 1], 2, k)
+
+    own3 = pl.ds(pl.multiple_of(z * bit, bit), bit)
+
+    def next2(k):
+        return copy(back4.at[own3], back4.at[own3], csend.at[k - 1], cback.at[k - 1], 2, k)
+
+    def next3(k):
+        return copy(final.at[c, d], final.at[c, d], fsend.at[k - 1], frecv.at[k - 1], 1, k)
+
+    def next4(k):
+        chip = lax.rem(c + k, 4)
+        return copy(final.at[chip, d], final.at[chip, d], gsend.at[k], grecv.at[chip], 0, 1)
+
+    wire3[...] = gq[pl.ds(pl.multiple_of((1 - column) * rest, rest), rest), :].astype(BF)
+    next0().start()
+    for h in range(4):
+        scatter(h, False)
+    next0().wait()
+    mine = gq[pl.ds(pl.multiple_of(column * rest, rest), rest), :] + got3[...].astype(F32)
+    sum3[...] = mine
+    wire3[...] = mine.astype(BF)
+    for k in range(1, planes):
+        next1(k).start()
+    for k in range(1, planes):
+        next1(k).wait()
+    mine = sum3[own3, :]
+    for k in range(planes - 1):
+        mine = mine + got4[k].astype(F32)
+    back4[own3, :] = mine.astype(BF)
+    for k in range(1, planes):
+        next2(k).start()
+
+    for b in range(4):
+        send_home(b, False)
+    for h in range(4):
+        own = jnp.logical_and(h == pair, native)
+
+        @pl.when(jnp.logical_not(own))
+        def _():
+            remote(dhome.at[h], dhome.at[h], hsems.at[h], hrecv.at[h], c, d).wait_recv()
+
+        for i in range(3):
+            first = i * width + 128 * h
+            dall[:, first : first + 128] = dhome[h, :, 128 * i : 128 * i + 128]
+
+    def input_rows(first, last):
+        @pl.loop(first, last)
+        def _(t):
+            rows = pl.ds(pl.multiple_of(t * 256, 256), 256)
+            x = x_ref[rows, :].astype(F32)
+            inv = lax.rsqrt(jnp.mean(x * x, axis=1, keepdims=True) + NORM_EPS)
+            normed = x * inv
+            scaled = dotf(dall[rows, :], w_ref[...], ((1,), (1,))) * gain_ref[...]
+            inner = jnp.mean(scaled * normed, axis=1, keepdims=True)
+            tg_ref[rows, :] = dres_ref[rows, :] + inv * (scaled - normed * inner)
+
+    count = x_ref.shape[0] // 256
+    input_rows(0, count // 2)
+    for k in range(1, planes):
+        next2(k).wait()
+    final[c, d] = back4[...]
+    for k in (2, 1, 3):
+        next3(k).start()
+    next4(0).start()
+    input_rows(count // 2, count)
+    for k in range(1, 4):
+        next3(k).wait_send()
+    for k in (1, 3, 2):
+        chip = lax.rem(c + 4 - k, 4)
+        copy(final.at[chip, d], final.at[chip, d], fsend.at[k - 1], frecv.at[k - 1], 1, k).wait_recv()
+        next4(4 - k).start()
+    for k in range(4):
+        next4(k).wait_send()
+    for chip in range(4):
+        copy(final.at[chip, 1 - d], final.at[chip, 1 - d], gsend.at[chip], grecv.at[chip], 0, 1).wait_recv()
+    for chip in range(4):
+        for e in range(2):
+            rows = slice((chip % 2) * rest, (chip % 2 + 1) * rest)
+            for i in range(3):
+                first = i * width + (2 * (chip // 2) + e) * 128
+                oq_ref[rows, first : first + 128] = final[chip, e, :, 128 * i : 128 * i + 128].astype(F32)
+    weighted = oq_ref[...] * w_ref[...].astype(F32)
+    gg_ref[...] = (
+        dotf(jnp.ones((8, weighted.shape[1]), F32), weighted, ((1,), (1,)), precision=lax.Precision.HIGHEST)
+        / gain_ref[...]
+    )
+
+
+def back_pass(d_att, qkv, o, lse, act, x, gain, w, d_res, g_proj, small, planes):
     length = qkv.shape[0]
+    count, width = x.shape
+    half = width // 2
+    eighth = half // 4
+    rest = width // 2
+    most = max(4, planes)
+    dma = pltpu.SemaphoreType.DMA
     return pl.pallas_call(
-        attention_back_kernel,
-        out_shape=jax.ShapeDtypeStruct((length, 384), BF),
-        in_specs=[VMEM] * 4,
-        out_specs=VMEM,
+        functools.partial(back_kernel, planes),
+        out_shape=(
+            jax.ShapeDtypeStruct((count, width), F32),
+            jax.ShapeDtypeStruct((width, 3 * width), F32),
+            jax.ShapeDtypeStruct((width, width), F32),
+            jax.ShapeDtypeStruct(small.shape, F32),
+            jax.ShapeDtypeStruct((8, width), F32),
+        ),
+        in_specs=[VMEM] * 11,
+        out_specs=(VMEM,) * 5,
         scratch_shapes=[
+            pltpu.VMEM((4, count, 128), BF),
             pltpu.VMEM((2, length, 128), BF),
             pltpu.VMEM((2, length, 128), BF),
             pltpu.VMEM((2, 128, length), BF),
             pltpu.VMEM((128, length), F32),
+            pltpu.VMEM((length, 256), F32),
             pltpu.VMEM((8, length), F32),
+            pltpu.VMEM((4, count, 384), BF),
+            pltpu.VMEM((4, count, 384), BF),
+            pltpu.VMEM((width, 384), F32),
+            pltpu.VMEM((count, 3 * width), BF),
+            pltpu.VMEM((half, width), BF),
+            pltpu.VMEM((half, width), BF),
+            pltpu.VMEM((half, width), BF),
+            pltpu.VMEM((3, eighth, width), BF),
+            pltpu.VMEM((planes, eighth, width), BF),
+            pltpu.VMEM((half, width), F32),
+            pltpu.VMEM((2, half, width), BF),
+            pltpu.VMEM((3, most) + small.shape, F32),
+            pltpu.VMEM((rest, 384), BF),
+            pltpu.VMEM((rest, 384), BF),
+            pltpu.VMEM((rest, 384), F32),
+            pltpu.VMEM((planes - 1, rest // planes, 384), BF),
+            pltpu.VMEM((rest, 384), BF),
+            pltpu.VMEM((4, 2, rest, 384), BF),
+            dma((2,)), dma((4,)), dma((4,)), dma((4,)), dma((4,)),
+            dma, dma((3,)), dma((planes - 1,)),
+            dma, dma((3,)), dma((planes - 1,)),
+            dma, dma((3,)),
+            dma((3, most - 1)), dma((3, most - 1)),
+            dma, dma, dma((planes - 1,)), dma((planes - 1,)), dma((planes - 1,)),
+            dma((3,)), dma((3,)), dma((4,)), dma((4,)),
         ],
-        compiler_params=params(),
-        name="attention_back",
-    )(qkv, do, o, lse)
+        compiler_params=params(collective_id=2, has_side_effects=True),
+        name="back_pass",
+    )(d_att, qkv, o, lse, act, x, gain, w, d_res, g_proj, small)
 
 
 def mix_kernel(
@@ -660,203 +943,6 @@
     gproj_ref[...] = dotf(att[...], dproj[...], ((0,), (0,)))
 
 
-def input_back_kernel(
-    dqkv_ref, x_ref, gain_ref, w_ref, dres_ref, tg_ref, gq_ref, gg_ref, act, dqkv
-):
-    tokens, width = x_ref.shape
-    for h in range(4):
-        for i in range(3):
-            first = i * width + 128 * h
-            dqkv[:, first : first + 128] = dqkv_ref[h, :, 128 * i : 128 * i + 128]
-    gain_grad = jnp.zeros((1, width), F32)
-    for t in range(tokens // 256):
-        rows = slice(t * 256, t * 256 + 256)
-        x = x_ref[rows, :].astype(F32)
-        inv = lax.rsqrt(jnp.mean(x * x, axis=1, keepdims=True) + NORM_EPS)
-        normed = x * inv
-        act[rows, :] = (normed * gain_ref[...]).astype(BF)
-        d_act = dotf(dqkv[rows, :], w_ref[...], ((1,), (1,)))
-        scaled = d_act * gain_ref[...]
-        gain_grad = gain_grad + jnp.sum(d_act * normed, axis=0, keepdims=True)
-        inner = jnp.mean(scaled * normed, axis=1, keepdims=True)
-        tg_ref[rows, :] = dres_ref[rows, :] + inv * (scaled - normed * inner)
-    gg_ref[...] = gain_grad
-    for i in range(3):
-        cols = slice(i * width, i * width + width)
-        gq_ref[i] = dotf(act[...], dqkv[:, cols], ((0,), (0,)))
-
-
-def reduce_kernel(
-    planes, experts,
-    gq_ref, gp_ref, small_ref, extra_ref,
-    oq_ref, op_ref, os_ref,
-    acc, wire, got0, got1, got2, quarter, gathered, half, slots,
-    send0, send1, send2, recv0, recv1, recv2, back0, back1, back2, ssend, srecv,
-):
-    z = lax.axis_index("experts")
-    c, d = coords()
-    width = gp_ref.shape[0]
-    eighth = got1.shape[1]
-    piece = got2.shape[1]
-    counts = (2, 4, planes)
-    places = (d, c, z)
-    axes = ("dp", "context", "experts")
-    barrier = pltpu.get_barrier_semaphore()
-
-    def mate(stage, k):
-        return {axes[stage]: lax.rem(places[stage] + k, counts[stage])}
-
-    total = 0
-    for stage in range(3):
-        for k in range(1, counts[stage]):
-            pl.semaphore_signal(barrier, inc=1, device_id=mate(stage, k), device_id_type=MESH)
-            total += 1
-    pl.semaphore_wait(barrier, total)
-
-    def copy(src, dst, send, recv, stage, k):
-        return pltpu.make_async_remote_copy(
-            src_ref=src, dst_ref=dst, send_sem=send, recv_sem=recv,
-            device_id=mate(stage, k), device_id_type=MESH,
-        )
-
-    def small_start(stage, value):
-        slots[stage, places[stage]] = value
-        own = slots.at[stage, places[stage]]
-        ops = [
-            copy(own, own, ssend.at[stage, k - 1], srecv.at[stage, k - 1], stage, k)
-            for k in range(1, counts[stage])
-        ]
-        for op in ops:
-            op.start()
-        return ops
-
-    def small_sum(stage, ops):
-        for op in ops:
-            op.wait()
-        value = slots[stage, 0]
-        for k in range(1, counts[stage]):
-            value = value + slots[stage, k]
-        return value
-
-    for i in range(4):
-        source = gq_ref.at[i] if i < 3 else gp_ref
-        rows = pl.ds((i % 2) * width, width)
-
-        @pl.when(d == i // 2)
-        def _():
-            acc[rows, :] = source[...]
-
-        @pl.when(d != i // 2)
-        def _():
-            wire[rows, :] = source[...].astype(BF)
-
-    first = copy(wire, got0, send0, recv0, 0, 1)
-    first.start()
-    which = lax.broadcasted_iota(jnp.int32, small_ref.shape, 0)
-    small = small_ref[...] + jnp.where(which == experts + 1, extra_ref[...], 0.0)
-    small_ops = small_start(0, small)
-    first.wait()
-    acc[...] = acc[...] + got0[...].astype(F32)
-
-    wire[...] = acc[...].astype(BF)
-    ops = []
-    for k in (2, 1, 3):
-        other = lax.rem(c + k, 4)
-        op = copy(
-            wire.at[pl.ds(other * eighth, eighth)], got1.at[k - 1], send1.at[k - 1], recv1.at[k - 1], 1, k
-        )
-        op.start()
-        ops.append(op)
-    small_ops = small_start(1, small_sum(0, small_ops))
-    for op in ops:
-        op.wait()
-    mine = acc[pl.ds(pl.multiple_of(c * eighth, eighth), eighth), :]
-    for k in range(3):
-        mine = mine + got1[k].astype(F32)
-    acc[0:eighth, :] = mine
-    quarter[...] = mine.astype(BF)
-    ops = []
-    for k in range(1, planes):
-        other = lax.rem(z + k, planes)
-        op = copy(
-            quarter.at[pl.ds(other * piece, piece)], got2.at[k - 1], send2.at[k - 1], recv2.at[k - 1], 2, k
-        )
-        op.start()
-        ops.append(op)
-    small_ops = small_start(2, small_sum(1, small_ops))
-    for op in ops:
-        op.wait()
-    mine = acc[pl.ds(pl.multiple_of(z * piece, piece), piece), :]
-    for k in range(planes - 1):
-        mine = mine + got2[k].astype(F32)
-
-    own = pl.ds(pl.multiple_of(z * piece, piece), piece)
-    plane_own = pl.ds(pl.multiple_of(c * eighth, eighth), eighth)
-    gathered[own, :] = mine.astype(BF)
-    ops = []
-    for k in range(1, planes):
-        op = copy(gathered.at[own], gathered.at[own], send2.at[k - 1], back2.at[k - 1], 2, k)
-        op.start()
-        ops.append(op)
-    os_ref[...] = small_sum(2, small_ops)
-    for op in ops:
-        op.wait()
-
-    half[d, plane_own, :] = gathered[...]
-    ops = []
-    for k in (2, 1, 3):
-        op = copy(half.at[d, plane_own], half.at[d, plane_own], send1.at[k - 1], back1.at[k - 1], 1, k)
-        op.start()
-        ops.append(op)
-    for op in ops:
-        op.wait()
-
-    last = copy(half.at[d], half.at[d], send0, back0, 0, 1)
-    last.start()
-    last.wait()
-    for i in range(4):
-        value = half[i // 2, (i % 2) * width : (i % 2 + 1) * width, :].astype(F32)
-        if i < 3:
-            oq_ref[:, i * width : (i + 1) * width] = value
-        else:
-            op_ref[...] = value
-
-
-def reduce_all(gq, gp, small, extra, planes, experts):
-    width = gp.shape[0]
-    eighth = width // 2
-    piece = eighth // planes
-    most = max(4, planes)
-    dma = pltpu.SemaphoreType.DMA
-    return pl.pallas_call(
-        functools.partial(reduce_kernel, planes, experts),
-        out_shape=(
-            jax.ShapeDtypeStruct((width, 3 * width), F32),
-            jax.ShapeDtypeStruct((width, width), F32),
-            jax.ShapeDtypeStruct(small.shape, F32),
-        ),
-        in_specs=[VMEM] * 4,
-        out_specs=(VMEM,) * 3,
-        scratch_shapes=[
-            pltpu.VMEM((2 * width, width), F32),
-            pltpu.VMEM((2 * width, width), BF),
-            pltpu.VMEM((2 * width, width), BF),
-            pltpu.VMEM((3, eighth, width), BF),
-            pltpu.VMEM((planes - 1, piece, width), BF),
-            pltpu.VMEM((eighth, width), BF),
-            pltpu.VMEM((eighth, width), BF),
-            pltpu.VMEM((2, 2 * width, width), BF),
-            pltpu.VMEM((3, most) + small.shape, F32),
-            dma, dma((3,)), dma((planes - 1,)),
-            dma, dma((3,)), dma((planes - 1,)),
-            dma, dma((3,)), dma((planes - 1,)),
-            dma((3, most - 1)), dma((3, most - 1)),
-        ],
-        compiler_params=params(collective_id=5, has_side_effects=True),
-        name="reduce_all",
-    )(gq, gp, small, extra)
-
-
 def pick_rows(sources, local, capacity, stride):
     pick = np.zeros((local, sources * capacity, sources * stride), np.float32)
     for e in range(local):
@@ -897,7 +983,7 @@
     pair_table = jnp.stack([group_routes.reshape(-1), route_order.reshape(-1)])
 
     sequence = gather_tokens(x, 4).reshape(4 * count, width)
-    qkv, o, lse = attention(sequence, gain_one, query_key_value_weight)
+    qkv, o, lse, act = attention(sequence, gain_one, query_key_value_weight)
     att = to_home(o.reshape(4, count, 128), 1)
 
     res, mix, weights, place, send = pl.pallas_call(
@@ -948,28 +1034,14 @@
         res, mix, weights, place, ret, gout, att, output_weight, gain_two, router_weight, pair_table
     )
 
-    d_o = to_heads(d_att, 2).reshape(4 * count, 128)
-    d_heads = attention_back(qkv, d_o, o, lse)
-    d_qkv = to_home(d_heads.reshape(4, count, 384), 3)
-    token_grad, g_qkv, g_one = pl.pallas_call(
-        input_back_kernel,
-        out_shape=(
-            jax.ShapeDtypeStruct((count, width), F32),
-            jax.ShapeDtypeStruct((3, width, width), F32),
-            jax.ShapeDtypeStruct((1, width), F32),
-        ),
-        in_specs=[VMEM] * 5,
-        out_specs=(VMEM,) * 3,
-        scratch_shapes=[pltpu.VMEM((count, width), BF), pltpu.VMEM((count, 3 * width), BF)],
-        compiler_params=params(),
-        name="input_back",
-    )(d_qkv, x, gain_one, query_key_value_weight, d_res)
+    token_grad, qkv_grad, proj_grad, small, g_one = back_pass(
+        d_att, qkv, o, lse, act, x, gain_one, query_key_value_weight, d_res, g_proj, small, planes
+    )
     g_in, g_out = expert_grads(all_rows, w_in, w_exp_out)
-    qkv_grad, proj_grad, small = reduce_all(g_qkv, g_proj, small, g_one, planes, experts)
     return (
         layer_out[None],
         token_grad[None],
-        small[experts + 1],
+        g_one[0],
         small[experts],
         qkv_grad,
         proj_grad,

time: 374 us -> 320 us (0.86)
  Pallas kernels: 322 us -> 265 us
  local copies, waits for them, and re-layouts: 8.85 us -> 12.7 us
    pallas_call x2 -> x1, Pallas kernels: 54.8 us -> 15.6 us  [to_home(): pl.pallas_call(home_kernel, out_shape=jax.ShapeDtypeStruct(x.shape, x.dty...]
    pallas_call x4 -> x1, Pallas kernels: 141 us -> 124 us  [back_pass(): pl.pallas_call(functools.partial(back_kernel, planes), out_shape=(jax.Sha...]
    unnamed x9 -> x12, local copies, waits for them, and re-layouts: 5.94 us -> 8.59 us
  transfers between devices with their start and end apart: 1 -> 1, of which waited for: 0 -> 0; matrix products, arithmetic and copies ran while one was open for 1% -> 1% of each run, Pallas kernels for 51% -> 41%
where the time goes in v2:
time: 320 us; the launch traced here: 319 us
  Pallas kernels  265 us (83%)
  blocking collectives  26.9 us (8%)
  between operations  14.1 us (4%)
  local copies, waits for them, and re-layouts  12.7 us (4%)
    pallas_call x1, Pallas kernels, back_pass(): pl.pallas_call(functools.partial(back_kernel, planes), out_shape=(jax.Sha...  124 us
    pallas_call x1, Pallas kernels, attention(): pl.pallas_call(attention_kernel, out_shape=(jax.ShapeDtypeStruct((length,...  39.1 us
    pallas_call x1, Pallas kernels, gather_tokens(): pl.pallas_call(gather_kernel, out_shape=jax.ShapeDtypeStruct((context,) +...  36.9 us
    pallas_call x1, Pallas kernels, expert_grads(): pl.pallas_call(expert_grad_kernel, grid=(local, hidden // chunk), out_sha...  24.1 us
    pallas_call x1, Pallas kernels, to_home(): pl.pallas_call(home_kernel, out_shape=jax.ShapeDtypeStruct(x.shape, x.dty...  15.6 us
    all_to_all x1, blocking collectives, per_device(): lax.all_to_all(send.reshape(sources, stride, 2 * width), 'experts', split...  13.8 us
    all_to_all x1, blocking collectives, per_device(): lax.all_to_all(ret.reshape(sources, stride, 2 * width), 'experts', split_...  13.1 us
    pallas_call x1, Pallas kernels, expert_rows(): pl.pallas_call(functools.partial(expert_kernel, steps), grid=(local, step...  10.8 us
  transfers between devices with their start and end apart: 1, of which 0 were waited for; matrix products, arithmetic and copies ran while one was open for 1% of the time, Pallas kernels for 41%

profile of v2, /device:TPU:0, one launch (start us, length us, event | category | flops | bytes accessed | tf_op | source)
XLA Modules:
  0.0 318.9 jit_solution(15462803557928051575)
XLA Ops:
  7.2 0.8 copy.30
  8.0 0.1 stack_reshape.6
  8.1 0.8 copy.31
  8.9 0.1 stack_reshape.7
  9.0 1.5 copy.32.router_ref
  10.5 36.9 %shard_map.196 = bf16[4,1024,512]{2,1,0:T(8,128)(2,1)} custom-call(bf16[1024,512]{1,0:T(8,128)(2,1)} %bitcast.18), custom_call_target="tpu_custom_call" | custom-call | tf_op jit(solution)/shard_map/pallas_call | solution.py:126
  47.4 39.1 %attention.1 = (bf16[4096,384]{1,0:T(8,128)(2,1)}, bf16[4096,128]{1,0:T(8,128)(2,1)}, f32[2,4096]{1,0:T(2,128)}, bf16[4096,512]{1,0:T(8,128)(2,1)}) custom-call(bf16[4096,512]{1,0:T(8,128)(2,1)} %bitcast.17, f32[1,512]{1,0:T(1,128)} %bitcast.31, bf16[512,1536]{1,0:T(8,128)(2,1)} %w_ref.3), custom_call_target="tpu_custom_call" | custom-call | tf_op jit(solution)/shard_map/attention/pallas_call | solution.py:267
  86.5 15.6 %shard_map.197.att_ref = bf16[4,1024,128]{2,1,0:T(8,128)(2,1)} custom-call(bf16[4,1024,128]{2,1,0:T(8,128)(2,1)} %bitcast.21), custom_call_target="tpu_custom_call" | custom-call | tf_op jit(solution)/shard_map/pallas_call | solution.py:182
  102.1 0.6 pad_add_fusion.pair_ref
  102.6 6.2 %mix.1 = (f32[1024,512]{1,0:T(8,128)}, bf16[1024,512]{1,0:T(8,128)(2,1)}, f32[128,1024]{1,0:T(8,128)}, bf16[192,128]{1,0:T(8,128)(2,1)}, bf16[192,1024]{1,0:T(8,128)(2,1)}) custom-call(bf16[1024,512]{1,0:T(8,128)(2,1)} %bitcast.19, bf16[4,1024,128]{2,1,0:T(8,128)(2,1)} %shard_map.197.att_ref, bf16[512,512]{1,0:T(8,128)(2,1)} %wo_ref.3, f32[1,512]{1,0:T(1,128)} %bitcast.29, ...), custom_call_target="tpu_custom_call" | custom-call | tf_op jit(solution)/shard_map/mix/pallas_call | solution.py:989
  108.8 13.8 %all_to_all.10 = bf16[4,48,1024]{2,1,0:T(8,128)(2,1)} all-to-all(bf16[4,48,1024]{2,1,0:T(8,128)(2,1)} %bitcast.28), channel_id=1, replica_groups=mesh['experts'=4,'context'=4,'dp'=2] {'experts'}, dimensions={0} | all-to-all | bytes 786432 | tf_op jit(solution)/shard_map/all_to_all | solution.py:1005
  122.6 10.8 %expert_rows.1 = (bf16[2,80,1024]{2,1,0:T(8,128)(2,1)}, bf16[192,1024]{1,0:T(8,128)(2,1)}) custom-call(bf16[192,1024]{1,0:T(8,128)(2,1)} %bitcast.25, bf16[2,80,192]{2,1,0:T(8,128)(2,1)} %constant.2.clone.pick_ref, bf16[2,512,2048]{2,1,0:T(8,128)(2,1)} %win_ref.3, bf16[2,2048,512]{2,1,0:T(8,128)(2,1)} %wout_ref.3), custom_call_target="tpu_custom_call" | custom-call | tf_op jit(solution)/shard_map/expert_rows/pallas_call | solution.py:814
  133.5 13.1 %all_to_all.11 = bf16[4,48,1024]{2,1,0:T(8,128)(2,1)} all-to-all(bf16[4,48,1024]{2,1,0:T(8,128)(2,1)} %bitcast.27), channel_id=1, replica_groups=mesh['experts'=4,'context'=4,'dp'=2] {'experts'}, dimensions={0} | all-to-all | bytes 786432 | tf_op jit(solution)/shard_map/all_to_all | solution.py:1010
  146.6 8.4 %unmix.1 = (bf16[1024,512]{1,0:T(8,128)(2,1)}, f32[1024,512]{1,0:T(8,128)}, bf16[4,1024,128]{2,1,0:T(8,128)(2,1)}, f32[512,512]{1,0:T(8,128)}, f32[16,512]{1,0:T(8,128)}) custom-call(f32[1024,512]{1,0:T(8,128)} %get-tuple-element.33.res_ref, bf16[1024,512]{1,0:T(8,128)(2,1)} %get-tuple-element.34.mix_ref, f32[128,1024]{1,0:T(8,128)} %get-tuple-element.35.wts_ref, ...), custom_call_target="tpu_custom_call" | custom-call | tf_op jit(solution)/shard_map/unmix/pallas_call | solution.py:1015
  155.0 123.5 %back_pass.1 = (f32[1024,512]{1,0:T(8,128)}, f32[512,1536]{1,0:T(8,128)}, f32[512,512]{1,0:T(8,128)}, f32[16,512]{1,0:T(8,128)}, f32[8,512]{1,0:T(8,128)}) custom-call(bf16[4,1024,128]{2,1,0:T(8,128)(2,1)} %get-tuple-element.40.datt_ref, bf16[4096,384]{1,0:T(8,128)(2,1)} %get-tuple-element.41.qkv_ref, bf16[4096,128]{1,0:T(8,128)(2,1)} %get-tuple-element.32.o_ref, ...), custom_call_target="tpu_custom_call" | custom-call | tf_op jit(solution)/shard_map/back_pass/pallas_call | solution.py:660
  278.5 1.3 slice.9
  279.8 1.3 slice.10
  281.1 1.3 slice_bitcast_fusion
  282.4 24.1 %expert_grads.1 = (f32[2,512,2048]{2,1,0:T(8,128)}, f32[2,2048,512]{2,1,0:T(8,128)}) custom-call(bf16[8,2,80,1024]{3,2,1,0:T(8,128)(2,1)} %bitcast.35, bf16[2,512,2048]{2,1,0:T(8,128)(2,1)} %win_ref.3, bf16[2,2048,512]{2,1,0:T(8,128)(2,1)} %wout_ref.3), custom_call_target="tpu_custom_call" | custom-call | flops 10737418240 | bytes 25165824 | tf_op jit(solution)/shard_map/expert_grads/pallas_call | solution.py:857
  306.5 1.3 copy.37
  307.8 1.3 copy-done
  309.2 1.7 copy.38
  310.8 0.3 copy-done.2
  311.1 1.0 copy.39
  (7 shorter events, 0.1 us)
Async XLA Ops:
  7.2 275.3 %all-gather.3.cloned.1.call-start = ((), (), s32[]{:S(2)}) async-start(), calls=%async_computation.2 | async-start | bytes 2949120 | tf_op jit(solution)/shard_map/all_gather | solution.py:1013
  282.4 24.1 %copy-start.1 = (f32[1024,512]{1,0:T(8,128)S(1)}, f32[1024,512]{1,0:T(8,128)}, u32[]{:S(2)}) copy-start(f32[1024,512]{1,0:T(8,128)} %get-tuple-element.47) | copy-start | bytes 6291460
  306.5 2.6 copy-start
  309.2 2.0 copy-start.2
Sparse Core Ops, SparseCore 0:
  133.6 30.1 all-gather.2

commit v3 on v2

--- a/solution.py
+++ b/solution.py
@@ -64,28 +64,47 @@
     )
 
 
-def gather_kernel(x_ref, g_ref, local, full_s, full_r, s1, s2, hr, fs, fr):
+def forward_kernel(
+    x_ref, gain_ref, w_ref,
+    att_ref, qkv_out, o_out, act_out, lse_ref,
+    g, ws, qkv, qh, vx, acc, peak, o, act,
+    local, full_s, full_r, s1, s2, hr, fs, fr, hsems, hrecv, outs,
+):
     c, d = coords()
     seq = sequence_of(c)
-    half = x_ref.shape[0] // 2
+    column = lax.rem(c, 2)
+    row = c // 2
+    pair = 2 * row + d
+    native = d == seq
+    block, width = x_ref.shape
+    half = block // 2
+
+    def at_phase(p):
+        return 2 * lax.rem(row + p // 2, 2) + lax.rem(column + lax.rem(p, 2), 2)
+
+    side, over, far = at_phase(1), at_phase(2), at_phase(3)
     plane_barrier(c, d)
-    native = d == seq
-    far = 3 - c
-    side = 2 * (c // 2) + 1 - lax.rem(c, 2)
-    over = 2 * (1 - c // 2) + lax.rem(c, 2)
 
     def part(ref, e):
         return ref.at[pl.ds(e * half, half)]
 
     def send(target, e, sem, slot):
-        return remote(part(x_ref, e), part(g_ref.at[c], e), sem.at[e], hr.at[slot], target, e)
+        return remote(part(x_ref, e), part(g.at[c], e), sem.at[e], hr.at[slot], target, e)
+
+    def whole():
+        return remote(x_ref, g.at[c], full_s, full_r, c, 1 - d)
+
+    def keep():
+        return pltpu.make_async_copy(x_ref, g.at[c], local.at[0])
+
+    def pass_on(slot, source, e):
+        mine = part(g.at[source], e)
+        return remote(mine, mine, fs.at[slot], fr.at[slot], c, 1 - d)
 
     @pl.when(native)
     def _():
-        for e in range(2):
-            send(far, e, s1, 0).start()
-        remote(x_ref, g_ref.at[c], full_s, full_r, c, 1 - d).start()
-        pltpu.make_async_copy(x_ref, g_ref.at[c], local).start()
+        keep().start()
+        whole().start()
 
     @pl.when(jnp.logical_not(native))
     def _():
@@ -93,207 +112,227 @@
             send(side, e, s1, 1).start()
             send(over, e, s2, 2).start()
 
-    forward = []
-    for slot, source in ((1, side), (2, over), (0, far)):
-        mine = part(g_ref.at[source], d)
-        remote(mine, mine, s1.at[0], hr.at[slot], c, d).wait_recv()
-        copy = remote(mine, mine, fs.at[slot], fr.at[slot], c, 1 - d)
-        copy.start()
-        forward.append(copy)
+    low = lax.broadcasted_iota(jnp.int32, (1, 128), 1) < 64
+    for i in range(3):
+        ws[:, 128 * i : 128 * i + 128] = w_ref[
+            :, pl.ds(pl.multiple_of(i * width + pair * 128, 128), 128)
+        ]
+
+    def project(b):
+        @pl.loop(0, block // TILE)
+        def _(t):
+            rows = pl.ds(pl.multiple_of(b * block + t * TILE, TILE), TILE)
+            x = g[b, pl.ds(pl.multiple_of(t * TILE, TILE), TILE), :].astype(F32)
+            inv = lax.rsqrt(jnp.mean(x * x, axis=1, keepdims=True) + NORM_EPS)
+            low_act = (x * inv * gain_ref[...]).astype(BF)
+            act[rows, :] = low_act
+            value = dotf(low_act, ws[...]).astype(BF)
+            q = value[:, 0:128] * jnp.asarray(0.125, BF)
+            zero = jnp.zeros_like(q)
+            qkv[rows, 0:128] = q
+            qkv[rows, 128:384] = value[:, 128:384]
+            qh[0, rows, :] = jnp.where(low, q, zero)
+            qh[1, rows, :] = jnp.where(low, zero, q)
+            vt = jnp.transpose(value[:, 256:384].astype(F32)).astype(BF)
+            for h in range(2):
+                vx[h, 0:64, rows] = vt[64 * h : 64 * h + 64, :]
+                vx[h, 64:80, rows] = jnp.ones((16, TILE), BF)
+                acc[h, :, rows] = jnp.zeros((80, TILE), F32)
+                peak[h : h + 1, rows] = jnp.full((1, TILE), MASKED, F32)
+        rows = pl.ds(pl.multiple_of(b * block, block), block)
+        pltpu.make_async_copy(qkv.at[rows], qkv_out.at[rows], outs.at[0, b]).start()
+        pltpu.make_async_copy(act.at[rows], act_out.at[rows], outs.at[1, b]).start()
+
+    def attend(qb, kb, first_key, first_query, keys, masked):
+        count = block - first_query
+        krows = pl.ds(pl.multiple_of(kb * block + first_key, keys), keys)
+        qrows = pl.ds(pl.multiple_of(qb * block + first_query, 256), count)
+        k = qkv[krows, 128:256]
+        scores = [dotf(k, qh[h, qrows, :], ((1,), (1,))) for h in range(2)]
+        for h in range(2):
+            s = scores[h]
+            if masked:
+                kpos = lax.broadcasted_iota(jnp.int32, s.shape, 0)
+                qpos = lax.broadcasted_iota(jnp.int32, s.shape, 1)
+                s = jnp.where(kpos <= qpos, s, MASKED)
+            m = peak[h : h + 1, qrows]
+            mn = jnp.maximum(m, jnp.max(s, axis=0, keepdims=True))
+            p = jnp.exp(s - mn).astype(BF)
+            al = jnp.exp(m - mn)
+            acc[h, :, qrows] = acc[h, :, qrows] * al + dotf(vx[h, :, krows], p)
+            peak[h : h + 1, qrows] = mn
+
+    def home(b):
+        rows = pl.ds(pl.multiple_of(b * block, block), block)
+        return remote(o.at[rows], att_ref.at[pair], hsems.at[b], hrecv.at[pair], b, seq)
+
+    def home_own():
+        rows = pl.ds(pl.multiple_of(c * block, block), block)
+        return pltpu.make_async_copy(o.at[rows], att_ref.at[pair], local.at[1])
+
+    def finish(b):
+        @pl.loop(0, block // TILE)
+        def _(t):
+            rows = pl.ds(pl.multiple_of(b * block + t * TILE, TILE), TILE)
+            parts = []
+            for h in range(2):
+                total = acc[h, 64:65, rows]
+                parts.append(acc[h, 0:64, rows] / total)
+                lse_ref[h : h + 1, rows] = peak[h : h + 1, rows] + jnp.log(total)
+            o[rows, :] = jnp.transpose(jnp.concatenate(parts, axis=0)).astype(BF)
+        own = jnp.logical_and(b == c, native)
+
+        @pl.when(own)
+        def _():
+            home_own().start()
+
+        @pl.when(jnp.logical_not(own))
+        def _():
+            home(b).start()
+
+        rows = pl.ds(pl.multiple_of(b * block, block), block)
+        pltpu.make_async_copy(o.at[rows], o_out.at[rows], outs.at[2, b]).start()
+
+    last_phase = []
+    for b in range(4):
+        phase = at_phase(b)
+        last_phase.append(phase if b == 0 else jnp.maximum(last_phase[-1], phase))
+
+    def complete(b, p):
+        phase = jnp.where(
+            b < 2,
+            jnp.where(b == 0, last_phase[0], last_phase[1]),
+            jnp.where(b == 2, last_phase[2], last_phase[3]),
+        )
+        return phase == p
+
+    @pl.loop(0, 4)
+    def _(p):
+        b = at_phase(p)
+
+        @pl.when(jnp.logical_and(p == 0, native))
+        def _():
+            keep().wait()
+
+        @pl.when(jnp.logical_and(p == 0, jnp.logical_not(native)))
+        def _():
+            whole().wait_recv()
+
+        for k, slot in ((1, 1), (2, 2), (3, 0)):
+            @pl.when(p == k)
+            def _():
+                source = at_phase(k)
+                mine = part(g.at[source], d)
+                remote(mine, mine, s1.at[0], hr.at[slot], c, d).wait_recv()
+                pass_on(slot, source, d).start()
+                if k == 1:
+                    @pl.when(native)
+                    def _():
+                        for e in range(2):
+                            send(far, e, s1, 0).start()
+                pass_on(slot, source, 1 - d).wait_recv()
+
+        project(b)
+        for t in range(block // TILE):
+            attend(b, b, TILE * t, TILE * t, TILE, True)
+
+        @pl.loop(0, p)
+        def _(r):
+            other = at_phase(r)
+            qb = jnp.maximum(b, other)
+            kb = jnp.minimum(b, other)
+
+            attend(qb, kb, 0, 0, block, False)
+
+            @pl.when(jnp.logical_and(qb == other, complete(qb, p)))
+            def _():
+                finish(qb)
+
+        @pl.when(complete(b, p))
+        def _():
+            finish(b)
+
+    for b in range(4):
+        own = jnp.logical_and(b == c, native)
+
+        @pl.when(own)
+        def _():
+            home_own().wait()
+
+        @pl.when(jnp.logical_not(own))
+        def _():
+            home(b).wait_send()
+
+        rows = pl.ds(b * block, block)
+        pltpu.make_async_copy(qkv.at[rows], qkv_out.at[rows], outs.at[0, b]).wait()
+        pltpu.make_async_copy(act.at[rows], act_out.at[rows], outs.at[1, b]).wait()
+        pltpu.make_async_copy(o.at[rows], o_out.at[rows], outs.at[2, b]).wait()
 
     @pl.when(native)
     def _():
+        whole().wait_send()
         for e in range(2):
             send(far, e, s1, 0).wait_send()
-        remote(x_ref, g_ref.at[c], full_s, full_r, c, 1 - d).wait_send()
-        pltpu.make_async_copy(x_ref, g_ref.at[c], local).wait()
 
     @pl.when(jnp.logical_not(native))
     def _():
         for e in range(2):
             send(side, e, s1, 1).wait_send()
             send(over, e, s2, 2).wait_send()
-        remote(x_ref, g_ref.at[c], full_s, full_r, c, 1 - d).wait_recv()
-
-    for copy in forward:
-        copy.wait_send()
+
     for slot, source in ((1, side), (2, over), (0, far)):
-        theirs = part(g_ref.at[source], 1 - d)
-        remote(theirs, theirs, fs.at[slot], fr.at[slot], c, 1 - d).wait_recv()
-
-
-def gather_tokens(x, context):
+        pass_on(slot, source, d).wait_send()
+    for h in range(4):
+        own = jnp.logical_and(h == pair, native)
+
+        @pl.when(jnp.logical_not(own))
+        def _():
+            remote(att_ref.at[h], att_ref.at[h], hsems.at[h], hrecv.at[h], c, d).wait_recv()
+
+
+def forward_pass(x, gain, w):
+    count, width = x.shape
+    length = 4 * count
+    dma = pltpu.SemaphoreType.DMA
     return pl.pallas_call(
-        gather_kernel,
-        out_shape=jax.ShapeDtypeStruct((context,) + x.shape, x.dtype),
-        in_specs=[ANY],
-        out_specs=ANY,
+        forward_kernel,
+        out_shape=(
+            jax.ShapeDtypeStruct((4, count, 128), BF),
+            jax.ShapeDtypeStruct((length, 384), BF),
+            jax.ShapeDtypeStruct((length, 128), BF),
+            jax.ShapeDtypeStruct((length, width), BF),
+            jax.ShapeDtypeStruct((2, length), F32),
+        ),
+        in_specs=[VMEM] * 3,
+        out_specs=(VMEM, ANY, ANY, ANY, VMEM),
         scratch_shapes=[
-            pltpu.SemaphoreType.DMA,
-            pltpu.SemaphoreType.DMA,
-            pltpu.SemaphoreType.DMA,
-            pltpu.SemaphoreType.DMA((2,)),
-            pltpu.SemaphoreType.DMA((2,)),
-            pltpu.SemaphoreType.DMA((3,)),
-            pltpu.SemaphoreType.DMA((3,)),
-            pltpu.SemaphoreType.DMA((3,)),
+            pltpu.VMEM((4, count, width), BF),
+            pltpu.VMEM((width, 384), BF),
+            pltpu.VMEM((length, 384), BF),
+            pltpu.VMEM((2, length, 128), BF),
+            pltpu.VMEM((2, 80, length), BF),
+            pltpu.VMEM((2, 80, length), F32),
+            pltpu.VMEM((2, length), F32),
+            pltpu.VMEM((length, 128), BF),
+            pltpu.VMEM((length, width), BF),
+            dma((2,)), dma, dma, dma((2,)), dma((2,)), dma((3,)), dma((3,)), dma((3,)),
+            dma((4,)), dma((4,)), dma((3, 4)),
         ],
         compiler_params=params(collective_id=0, has_side_effects=True),
-    )(x)
-
-
-def home_kernel(x_ref, o_ref, local, send, recv):
-    c, e = coords()
-    seq = sequence_of(c)
-    pair = 2 * (c // 2) + e
-    plane_barrier(c, e)
-    for k in range(4):
-        b = lax.rem(c + 3 - k, 4)
-        own = jnp.logical_and(b == c, e == seq)
-
-        @pl.when(own)
-        def _():
-            pltpu.make_async_copy(x_ref.at[b], o_ref.at[pair], local).start()
-
-        @pl.when(jnp.logical_not(own))
-        def _():
-            remote(x_ref.at[b], o_ref.at[pair], send.at[b], recv.at[pair], b, seq).start()
-
-    for b in range(4):
-        own = jnp.logical_and(b == c, e == seq)
-
-        @pl.when(own)
-        def _():
-            pltpu.make_async_copy(x_ref.at[b], o_ref.at[pair], local).wait()
-
-        @pl.when(jnp.logical_not(own))
-        def _():
-            remote(x_ref.at[b], o_ref.at[pair], send.at[b], recv.at[pair], b, seq).wait_send()
-
-    for h in range(4):
-        own = jnp.logical_and(h == pair, e == seq)
-
-        @pl.when(jnp.logical_not(own))
-        def _():
-            remote(x_ref.at[h], o_ref.at[h], send.at[h], recv.at[h], c, e).wait_recv()
-
-
-def to_home(x, cid):
-    return pl.pallas_call(
-        home_kernel,
-        out_shape=jax.ShapeDtypeStruct(x.shape, x.dtype),
-        in_specs=[ANY],
-        out_specs=ANY,
-        scratch_shapes=[
-            pltpu.SemaphoreType.DMA,
-            pltpu.SemaphoreType.DMA((4,)),
-            pltpu.SemaphoreType.DMA((4,)),
-        ],
-        compiler_params=params(collective_id=cid, has_side_effects=True),
-    )(x)
-
-
-def attention_kernel(x_ref, gain_ref, w_ref, qkv_ref, o_ref, lse_ref, act_ref, ws, vx, acc):
-    length = x_ref.shape[0]
-    tq, tk = 1024, 512
-    c, e = coords()
-    pair = 2 * (c // 2) + e
-    lane = lax.broadcasted_iota(jnp.int32, (1, 128), 1)
-    low = lane < 64
-    width = w_ref.shape[0]
-    for i in range(3):
-        ws[:, 128 * i : 128 * i + 128] = w_ref[
-            :, pl.ds(pl.multiple_of(i * width + pair * 128, 128), 128)
-        ]
-
-    @pl.loop(0, length // TILE)
-    def _(t):
-        rows = pl.ds(pl.multiple_of(t * TILE, TILE), TILE)
-        x = x_ref[rows, :].astype(F32)
-        inv = lax.rsqrt(jnp.mean(x * x, axis=1, keepdims=True) + NORM_EPS)
-        act = (x * inv * gain_ref[...]).astype(BF)
-        act_ref[rows, :] = act
-        qkv = dotf(act, ws[...]).astype(BF)
-        qkv_ref[rows, 0:128] = qkv[:, 0:128] * jnp.asarray(0.125, BF)
-        qkv_ref[rows, 128:384] = qkv[:, 128:384]
-        vt = jnp.transpose(qkv[:, 256:384].astype(F32)).astype(BF)
-        for h in range(2):
-            vx[h, 0:64, rows] = vt[64 * h : 64 * h + 64, :]
-            vx[h, 64:80, rows] = jnp.ones((16, TILE), BF)
-
-    def step(i, j, qs, carry, diag):
-        krows = pl.ds(pl.multiple_of(j * tk, tk), tk)
-        k = qkv_ref[krows, 128:256]
-        out = []
-        first = 0 if diag is None else diag * tk
-        cols = slice(first, tq)
-        for h in range(2):
-            m = carry[h][:, cols]
-            s = dotf(k, qs[h][cols, :], ((1,), (1,)))
-            if diag is not None:
-                kpos = lax.broadcasted_iota(jnp.int32, s.shape, 0)
-                qpos = lax.broadcasted_iota(jnp.int32, s.shape, 1)
-                s = jnp.where(kpos <= qpos, s, MASKED)
-            mn = jnp.maximum(m, jnp.max(s, axis=0, keepdims=True))
-            p = jnp.exp(s - mn).astype(BF)
-            al = jnp.exp(m - mn)
-            acc[h, :, cols] = acc[h, :, cols] * al + dotf(vx[h, :, krows], p)
-            if first:
-                mn = jnp.concatenate([carry[h][:, :first], mn], axis=1)
-            out.append(mn)
-        return tuple(out)
-
-    @pl.loop(0, length // tq)
-    def _(i):
-        rows = pl.ds(pl.multiple_of(i * tq, tq), tq)
-        q = qkv_ref[rows, 0:128]
-        z = jnp.zeros_like(q)
-        qs = [jnp.where(low, q, z), jnp.where(low, z, q)]
-        acc[...] = jnp.zeros_like(acc)
-        m0 = jnp.full((1, tq), MASKED, F32)
-        carry = lax.fori_loop(0, i * (tq // tk), lambda j, m: step(i, j, qs, m, None), (m0, m0))
-        for t in range(tq // tk):
-            carry = step(i, i * (tq // tk) + t, qs, carry, t)
-        parts = []
-        for h in range(2):
-            total = acc[h, 64:65, :]
-            parts.append(acc[h, 0:64, :] / total)
-            lse_ref[h : h + 1, rows] = carry[h] + jnp.log(total)
-        o_ref[rows, :] = jnp.transpose(jnp.concatenate(parts, axis=0)).astype(BF)
-
-
-def attention(x, gain, w):
-    length = x.shape[0]
-    return pl.pallas_call(
-        attention_kernel,
-        out_shape=(
-            jax.ShapeDtypeStruct((length, 384), BF),
-            jax.ShapeDtypeStruct((length, 128), BF),
-            jax.ShapeDtypeStruct((2, length), F32),
-            jax.ShapeDtypeStruct(x.shape, BF),
-        ),
-        in_specs=[VMEM] * 3,
-        out_specs=(VMEM,) * 4,
-        scratch_shapes=[
-            pltpu.VMEM((w.shape[0], 384), BF),
-            pltpu.VMEM((2, 80, length), BF),
-            pltpu.VMEM((2, 80, 1024), F32),
-        ],
-        compiler_params=params(),
-        name="attention",
+        name="forward_pass",
     )(x, gain, w)
 
 
 def back_kernel(
     planes,
-    datt_ref, qkv_ref, o_ref, lse_ref, act_ref, x_ref, gain_ref, w_ref, dres_ref, gp_ref, small_ref,
-    tg_ref, oq_ref, op_ref, os_ref, gg_ref,
-    do, qh, dh, kh, dq, dkv, delta, dsend, dhome, gq, dall,
+    datt_ref, qkv_ref, o_ref, lse_ref, act_hbm, x_hbm, gain_ref, w_hbm, dres_hbm, gp_ref, small_ref,
+    tg_hbm, final_hbm, op_ref, os_ref, gg_ref,
+    act_ref, x_ref, w_ref, dres_ref, do, qh, dh, kh, dq, dkv, delta, dsend, dhome, gq, dall,
     wire0, got0, wire1, got1, all2, sum1, back1, slots,
     wire3, got3, sum3, got4, back4, final,
     local, dsems, drecv, hsems, hrecv,
     send0, send1, send2, recv0, recv1, recv2, ret0, ret1, ssend, srecv,
-    bsend, brecv, csend, crecv, cback, fsend, frecv, gsend, grecv,
+    bsend, brecv, csend, crecv, cback, fsend, frecv, gsend, grecv, loads, stores,
 ):
     z = lax.axis_index("experts")
     c, d = coords()
@@ -350,6 +389,15 @@
 
     for h in range(4):
         scatter(h, True)
+
+    late = [
+        pltpu.make_async_copy(source, target, loads.at[k])
+        for k, (source, target) in enumerate(
+            ((act_hbm, act_ref), (x_hbm, x_ref), (w_hbm, w_ref), (dres_hbm, dres_ref))
+        )
+    ]
+    for op in late:
+        op.start()
 
     low = lax.broadcasted_iota(jnp.int32, (1, 128), 1) < 64
     low_rows = lax.broadcasted_iota(jnp.int32, (128, 1), 0) < 64
@@ -510,6 +558,9 @@
         dkv[krows, 0:128] = dkv[krows, 0:128] + dk
         dkv[krows, 128:256] = dkv[krows, 128:256] + dv
 
+    for op in late:
+        op.wait()
+
     def send_home(b, go):
         own = jnp.logical_and(b == c, native)
 
@@ -615,7 +666,7 @@
             normed = x * inv
             scaled = dotf(dall[rows, :], w_ref[...], ((1,), (1,))) * gain_ref[...]
             inner = jnp.mean(scaled * normed, axis=1, keepdims=True)
-            tg_ref[rows, :] = dres_ref[rows, :] + inv * (scaled - normed * inner)
+            dres_ref[rows, :] = dres_ref[rows, :] + inv * (scaled - normed * inner)
 
     count = x_ref.shape[0] // 256
     input_rows(0, count // 2)
@@ -626,6 +677,8 @@
         next3(k).start()
     next4(0).start()
     input_rows(count // 2, count)
+    result = pltpu.make_async_copy(dres_ref, tg_hbm, loads.at[0])
+    result.start()
     for k in range(1, 4):
         next3(k).wait_send()
     for k in (1, 3, 2):
@@ -636,17 +689,36 @@
         next4(k).wait_send()
     for chip in range(4):
         copy(final.at[chip, 1 - d], final.at[chip, 1 - d], gsend.at[chip], grecv.at[chip], 0, 1).wait_recv()
+    spread = []
     for chip in range(4):
         for e in range(2):
-            rows = slice((chip % 2) * rest, (chip % 2 + 1) * rest)
             for i in range(3):
-                first = i * width + (2 * (chip // 2) + e) * 128
-                oq_ref[rows, first : first + 128] = final[chip, e, :, 128 * i : 128 * i + 128].astype(F32)
-    weighted = oq_ref[...] * w_ref[...].astype(F32)
-    gg_ref[...] = (
-        dotf(jnp.ones((8, weighted.shape[1]), F32), weighted, ((1,), (1,)), precision=lax.Precision.HIGHEST)
-        / gain_ref[...]
-    )
+                rows = pl.ds((chip % 2) * rest, rest)
+                cols = pl.ds(i * width + (2 * (chip // 2) + e) * 128, 128)
+                op = pltpu.make_async_copy(
+                    final.at[chip, e, :, pl.ds(128 * i, 128)],
+                    final_hbm.at[rows, cols],
+                    stores.at[len(spread)],
+                )
+                op.start()
+                spread.append(op)
+    for part in range(2):
+        rows = slice(part * rest, (part + 1) * rest)
+        weighted = 0.0
+        for row in range(2):
+            for e in range(2):
+                for i in range(3):
+                    first = i * width + (2 * row + e) * 128
+                    weighted = weighted + w_ref[rows, first : first + 128].astype(F32) * final[
+                        2 * row + part, e, :, 128 * i : 128 * i + 128
+                    ].astype(F32)
+        gg_ref[:, rows] = (
+            dotf(jnp.ones((8, 128), F32), weighted, ((1,), (1,)), precision=lax.Precision.HIGHEST)
+            / gain_ref[:, rows]
+        )
+    result.wait()
+    for op in spread:
+        op.wait()
 
 
 def back_pass(d_att, qkv, o, lse, act, x, gain, w, d_res, g_proj, small, planes):
@@ -661,14 +733,18 @@
         functools.partial(back_kernel, planes),
         out_shape=(
             jax.ShapeDtypeStruct((count, width), F32),
-            jax.ShapeDtypeStruct((width, 3 * width), F32),
+            jax.ShapeDtypeStruct((width, 3 * width), BF),
             jax.ShapeDtypeStruct((width, width), F32),
             jax.ShapeDtypeStruct(small.shape, F32),
             jax.ShapeDtypeStruct((8, width), F32),
         ),
-        in_specs=[VMEM] * 11,
-        out_specs=(VMEM,) * 5,
+        in_specs=[VMEM, VMEM, VMEM, VMEM, ANY, ANY, VMEM, ANY, ANY, VMEM, VMEM],
+        out_specs=(ANY, ANY, VMEM, VMEM, VMEM),
         scratch_shapes=[
+            pltpu.VMEM(act.shape, BF),
+            pltpu.VMEM(x.shape, BF),
+            pltpu.VMEM(w.shape, BF),
+            pltpu.VMEM(x.shape, F32),
             pltpu.VMEM((4, count, 128), BF),
             pltpu.VMEM((2, length, 128), BF),
             pltpu.VMEM((2, length, 128), BF),
@@ -700,7 +776,7 @@
             dma, dma((3,)),
             dma((3, most - 1)), dma((3, most - 1)),
             dma, dma, dma((planes - 1,)), dma((planes - 1,)), dma((planes - 1,)),
-            dma((3,)), dma((3,)), dma((4,)), dma((4,)),
+            dma((3,)), dma((3,)), dma((4,)), dma((4,)), dma((4,)), dma((24,)),
         ],
         compiler_params=params(collective_id=2, has_side_effects=True),
         name="back_pass",
@@ -834,26 +910,37 @@
     )(recv, pick, w_in, w_out)
 
 
-def expert_grad_kernel(rows_ref, win_ref, wout_ref, gin_ref, gout_ref, x, dy):
+def expert_grad_kernel(rows_ref, win_ref, wout_ref, gin_ref, gout_ref, xt, dy, dyt):
     width = win_ref.shape[1]
     copies, _, count, _ = rows_ref.shape
 
     @pl.when(pl.program_id(1) == 0)
     def _():
-        for k in range(copies):
-            x[k * count : (k + 1) * count, :] = rows_ref[k, 0, :, 0:width]
-            dy[k * count : (k + 1) * count, :] = rows_ref[k, 0, :, width:]
-
-    hidden, slope = gelu_parts(dotf(x[...], win_ref[0]))
-    d_pre = (dotf(dy[...], wout_ref[0], ((1,), (1,))) * slope).astype(BF)
-    gin_ref[0] = dotf(x[...], d_pre, ((0,), (0,)))
-    gout_ref[0] = dotf(hidden.astype(BF), dy[...], ((0,), (0,)))
+        x = jnp.concatenate([rows_ref[k, 0, :, 0:width] for k in range(copies)], axis=0)
+        xt[...] = jnp.transpose(x.astype(F32)).astype(BF)
+        value = jnp.concatenate([rows_ref[k, 0, :, width:] for k in range(copies)], axis=0)
+        dy[...] = value
+        dyt[...] = jnp.transpose(value.astype(F32)).astype(BF)
+
+    chunk = wout_ref.shape[1]
+    parts = [slice(0, chunk // 2), slice(chunk // 2, chunk)]
+    first = []
+    for part in parts:
+        win_t = jnp.transpose(win_ref[0, :, part].astype(F32)).astype(BF)
+        first.append((dotf(win_t, xt[...]), dotf(wout_ref[0, part, :], dyt[...])))
+    second = []
+    for pre, d_hidden in first:
+        hidden, slope = gelu_parts(pre)
+        second.append((hidden.astype(BF), (d_hidden * slope).astype(BF)))
+    for part, (hidden, d_pre) in zip(parts, second):
+        gin_ref[0, :, part] = dotf(xt[...], d_pre, ((1,), (1,)))
+        gout_ref[0, part, :] = dotf(hidden, dy[...])
 
 
 def expert_grads(rows, w_in, w_out):
     copies, local, count, double = rows.shape
     _, width, hidden = w_in.shape
-    chunk = 256
+    chunk = 512
     return pl.pallas_call(
         expert_grad_kernel,
         grid=(local, hidden // chunk),
@@ -871,8 +958,9 @@
             pl.BlockSpec((1, chunk, width), lambda e, f: (e, f, 0)),
         ),
         scratch_shapes=[
+            pltpu.VMEM((width, copies * count), BF),
             pltpu.VMEM((copies * count, width), BF),
-            pltpu.VMEM((copies * count, width), BF),
+            pltpu.VMEM((width, copies * count), BF),
         ],
         compiler_params=params(),
         cost_estimate=pl.CostEstimate(
@@ -982,9 +1070,7 @@
     gain_two = mix_gain.reshape(1, width)
     pair_table = jnp.stack([group_routes.reshape(-1), route_order.reshape(-1)])
 
-    sequence = gather_tokens(x, 4).reshape(4 * count, width)
-    qkv, o, lse, act = attention(sequence, gain_one, query_key_value_weight)
-    att = to_home(o.reshape(4, count, 128), 1)
+    att, qkv, o, act, lse = forward_pass(x, gain_one, query_key_value_weight)
 
     res, mix, weights, place, send = pl.pallas_call(
         functools.partial(mix_kernel, stride, capacity, local, choices),
@@ -1043,7 +1129,7 @@
         token_grad[None],
         g_one[0],
         small[experts],
-        qkv_grad,
+        qkv_grad.astype(F32),
         proj_grad,
         jnp.transpose(small[:experts]),
         g_in,

time: 320 us -> 287 us (0.90)
  Pallas kernels: 265 us -> 227 us
  blocking collectives: 26.9 us -> 30.4 us
  other arithmetic: 0.57 us -> 4.05 us
  local copies, waits for them, and re-layouts: 12.7 us -> 9.34 us
    pallas_call x3 -> x1, Pallas kernels: 91.6 us -> 62.7 us  [forward_pass(): pl.pallas_call(forward_kernel, out_shape=(jax.ShapeDtypeStruct((4, count,...]
    pallas_call x1, Pallas kernels: 124 us -> 118 us  [back_pass(): pl.pallas_call(functools.partial(back_kernel, planes), out_shape=(jax.Sha...]
    convert_element_type x0 -> x1, other arithmetic: none -> 3.48 us  [per_device(): qkv_grad.astype(F32)]
    unnamed x12 -> x11, local copies, waits for them, and re-layouts: 8.59 us -> 5.93 us
  transfers between devices with their start and end apart: 1 -> 1, of which waited for: 0 -> 0; matrix products, arithmetic and copies ran while one was open for 1% -> 2% of each run, Pallas kernels for 41% -> 44%
where the time goes in v3:
time: 287 us; the launch traced here: 284 us
  Pallas kernels  227 us (79%)
  blocking collectives  30.4 us (11%)
  between operations  14.1 us (5%)
  local copies, waits for them, and re-layouts  9.34 us (3%)
  other arithmetic  4.05 us (1%)
    pallas_call x1, Pallas kernels, back_pass(): pl.pallas_call(functools.partial(back_kernel, planes), out_shape=(jax.Sha...  118 us
    pallas_call x1, Pallas kernels, forward_pass(): pl.pallas_call(forward_kernel, out_shape=(jax.ShapeDtypeStruct((4, count,...  62.7 us
    pallas_call x1, Pallas kernels, expert_grads(): pl.pallas_call(expert_grad_kernel, grid=(local, hidden // chunk), out_sha...  20.9 us
    all_to_all x1, blocking collectives, per_device(): lax.all_to_all(send.reshape(sources, stride, 2 * width), 'experts', split...  15.8 us
    all_to_all x1, blocking collectives, per_device(): lax.all_to_all(ret.reshape(sources, stride, 2 * width), 'experts', split_...  14.6 us
    pallas_call x1, Pallas kernels, expert_rows(): pl.pallas_call(functools.partial(expert_kernel, steps), grid=(local, step...  10.8 us
    pallas_call x1, Pallas kernels, per_device(): pl.pallas_call(functools.partial(unmix_kernel, choices), out_shape=(jax.S...  8.4 us
    pallas_call x1, Pallas kernels, per_device(): pl.pallas_call(functools.partial(mix_kernel, stride, capacity, local, cho...  6.18 us
  transfers between devices with their start and end apart: 1, of which 0 were waited for; matrix products, arithmetic and copies ran while one was open for 2% of the time, Pallas kernels for 44%

profile of v3, /device:TPU:0, one launch (start us, length us, event | category | flops | bytes accessed | tf_op | source)
XLA Modules:
  0.0 284.5 jit_solution(16624527767427989050)
XLA Ops:
  7.2 0.0 all-gather.3.cloned.1.call-start
  7.2 0.8 copy.30
  8.0 0.1 stack_reshape.6
  8.1 0.8 copy.31
  8.9 0.1 stack_reshape.7
  9.0 1.5 copy.32.router_ref
  10.5 0.6 pad_add_fusion.pair_ref
  11.0 62.7 %forward_pass.1 = (bf16[4,1024,128]{2,1,0:T(8,128)(2,1)}, bf16[4096,384]{1,0:T(8,128)(2,1)}, bf16[4096,128]{1,0:T(8,128)(2,1)}, bf16[4096,512]{1,0:T(8,128)(2,1)}, f32[2,4096]{1,0:T(2,128)}) custom-call(bf16[1024,512]{1,0:T(8,128)(2,1)} %bitcast.15, f32[1,512]{1,0:T(1,128)} %bitcast.27, bf16[512,1536]{1,0:T(8,128)(2,1)} %w_hbm.1), custom_call_target="tpu_custom_call" | custom-call | tf_op jit(solution)/shard_map/forward_pass/pallas_call | solution.py:297
  73.7 6.2 %mix.1 = (f32[1024,512]{1,0:T(8,128)}, bf16[1024,512]{1,0:T(8,128)(2,1)}, f32[128,1024]{1,0:T(8,128)}, bf16[192,128]{1,0:T(8,128)(2,1)}, bf16[192,1024]{1,0:T(8,128)(2,1)}) custom-call(bf16[1024,512]{1,0:T(8,128)(2,1)} %bitcast.16, bf16[4,1024,128]{2,1,0:T(8,128)(2,1)} %get-tuple-element.33.att_ref, bf16[512,512]{1,0:T(8,128)(2,1)} %wo_ref.3, ...), custom_call_target="tpu_custom_call" | custom-call | tf_op jit(solution)/shard_map/mix/pallas_call | solution.py:1075
  79.9 15.8 %all_to_all.10 = bf16[4,48,1024]{2,1,0:T(8,128)(2,1)} all-to-all(bf16[4,48,1024]{2,1,0:T(8,128)(2,1)} %bitcast.24), channel_id=1, replica_groups=mesh['experts'=4,'context'=4,'dp'=2] {'experts'}, dimensions={0} | all-to-all | bytes 786432 | tf_op jit(solution)/shard_map/all_to_all | solution.py:1091
  95.7 10.8 %expert_rows.1 = (bf16[2,80,1024]{2,1,0:T(8,128)(2,1)}, bf16[192,1024]{1,0:T(8,128)(2,1)}) custom-call(bf16[192,1024]{1,0:T(8,128)(2,1)} %bitcast.21, bf16[2,80,192]{2,1,0:T(8,128)(2,1)} %constant.2.clone.pick_ref, bf16[2,512,2048]{2,1,0:T(8,128)(2,1)} %win_ref.3, bf16[2,2048,512]{2,1,0:T(8,128)(2,1)} %wout_ref.3), custom_call_target="tpu_custom_call" | custom-call | tf_op jit(solution)/shard_map/expert_rows/pallas_call | solution.py:890
  106.6 0.0 all-gather.3.cloned.1.call-update
  106.6 14.6 %all_to_all.11 = bf16[4,48,1024]{2,1,0:T(8,128)(2,1)} all-to-all(bf16[4,48,1024]{2,1,0:T(8,128)(2,1)} %bitcast.23), channel_id=1, replica_groups=mesh['experts'=4,'context'=4,'dp'=2] {'experts'}, dimensions={0} | all-to-all | bytes 786432 | tf_op jit(solution)/shard_map/all_to_all | solution.py:1096
  121.2 8.4 %unmix.1 = (bf16[1024,512]{1,0:T(8,128)(2,1)}, f32[1024,512]{1,0:T(8,128)}, bf16[4,1024,128]{2,1,0:T(8,128)(2,1)}, f32[512,512]{1,0:T(8,128)}, f32[16,512]{1,0:T(8,128)}) custom-call(f32[1024,512]{1,0:T(8,128)} %get-tuple-element.34.res_ref, bf16[1024,512]{1,0:T(8,128)(2,1)} %get-tuple-element.35.mix_ref, f32[128,1024]{1,0:T(8,128)} %get-tuple-element.36.wts_ref, ...), custom_call_target="tpu_custom_call" | custom-call | tf_op jit(solution)/shard_map/unmix/pallas_call | solution.py:1101
  129.6 117.5 %back_pass.1 = (f32[1024,512]{1,0:T(8,128)}, bf16[512,1536]{1,0:T(8,128)(2,1)}, f32[512,512]{1,0:T(8,128)}, f32[16,512]{1,0:T(8,128)}, f32[8,512]{1,0:T(8,128)}) custom-call(bf16[4,1024,128]{2,1,0:T(8,128)(2,1)} %get-tuple-element.41.datt_ref, bf16[4096,384]{1,0:T(8,128)(2,1)} %get-tuple-element.42.qkv_ref, bf16[4096,128]{1,0:T(8,128)(2,1)} %get-tuple-element.43.o_ref, ...), custom_call_target="tpu_custom_call" | custom-call | tf_op jit(solution)/shard_map/back_pass/pallas_call | solution.py:732
  247.1 0.0 copy-start.2
  247.1 1.3 slice.9
  248.4 1.3 slice.10
  249.7 3.5 %convert_element_type.3 = f32[512,1536]{1,0:T(8,128)} convert(bf16[512,1536]{1,0:T(8,128)(2,1)} %get-tuple-element.52) | non-fusion elementwise | flops 786432 | bytes 4718592 | tf_op jit(solution)/shard_map/convert_element_type | solution.py:1132
  253.2 0.6 slice_bitcast_fusion
  253.8 20.9 %expert_grads.1 = (f32[2,512,2048]{2,1,0:T(8,128)}, f32[2,2048,512]{2,1,0:T(8,128)}) custom-call(bf16[8,2,80,1024]{3,2,1,0:T(8,128)(2,1)} %bitcast.31, bf16[2,512,2048]{2,1,0:T(8,128)(2,1)} %win_ref.3, bf16[2,2048,512]{2,1,0:T(8,128)(2,1)} %wout_ref.3), custom_call_target="tpu_custom_call" | custom-call | flops 10737418240 | bytes 25165824 | tf_op jit(solution)/shard_map/expert_grads/pallas_call | solution.py:944
  274.7 1.3 copy.36
  276.1 0.6 copy-done.1
  276.7 1.0 copy.37
  (5 shorter events, 0.0 us)
Async XLA Ops:
  7.2 246.7 %all-gather.3.cloned.1.call-start = ((), (), s32[]{:S(2)}) async-start(), calls=%async_computation.2 | async-start | bytes 2949120 | tf_op jit(solution)/shard_map/all_gather | solution.py:1099
  247.1 6.1 %copy-start.2 = (f32[16,512]{1,0:T(8,128)S(1)}, f32[16,512]{1,0:T(8,128)}, u32[]{:S(2)}) copy-start(f32[16,512]{1,0:T(8,128)} %get-tuple-element.51) | copy-start | bytes 98308
  253.8 20.9 %copy-start = (f32[1024,512]{1,0:T(8,128)S(1)}, f32[1024,512]{1,0:T(8,128)}, u32[]{:S(2)}) copy-start(f32[1024,512]{1,0:T(8,128)} %get-tuple-element.49) | copy-start | bytes 6291460
  274.7 1.9 copy-start.1
Sparse Core Ops, SparseCore 0:
  106.7 31.6 all-gather.2
